TPU v7x, 32 devices: a whole 2x2x4 slice. The times are simulated.
32 devices in a mesh: wide: 8 (over z, y), section: 4 (over x, core).
Axes of the slice: x: 2, y: 2, z: 4, core: 2. Of those that a mesh axis runs over, the one named last changes fastest.
Arguments:
- tokens: bfloat16 [64, 16384], P('wide', 'section'), may hold values from -6 to 6
- gate_kept: bfloat16 [8192, 32768], P('section', 'wide'), may hold values from -0.0625 to 0.0625
- up_kept: bfloat16 [8192, 32768], P('section', 'wide'), may hold values from -0.0625 to 0.0625
- gate_keep: int32 [128, 32768], P('section', 'wide'), may hold values from 0 to 5
- up_keep: int32 [128, 32768], P('section', 'wide'), may hold values from 0 to 5
- down_weight: bfloat16 [32768, 16384], P('wide', 'section'), may hold values from -0.03125 to 0.03125
Outputs:
- next_input: bfloat16 [64, 16384], P('wide', 'section')
- gram: float32 [16384, 16384], P('section', 'wide')
Inputs may be any that keep to these rules, and one draw needn't show every extreme that they name: `gate_keep`: a pattern code names one of the six pairs of positions kept in each group of four input rows. `up_keep`: a pattern code names one of the six pairs of positions kept in each group of four input rows.
All inputs are finite; a program needn't handle non-finite values.
Results may differ from a plain program's by a relative error of at most 0.0063.
Values may be sent and summed in bfloat16 or wider, within the bound.
No kernel may reach another device: no remote copies, remote signals or barrier semaphores. Data moves between devices by JAX's collectives and lax.ppermute only.
A program may use at most 320 MiB of HBM per device.

v0:
```python
import math

import jax
import jax.numpy as jnp
from jax import lax
from jax.sharding import PartitionSpec as P


def from_root(value, axis, source):
    kept = jnp.where(lax.axis_index(axis) == source, value, 0).astype(value.dtype)
    return lax.psum(kept, axis)


def expand(kept, codes):
    blocks = codes.shape[0]
    width = kept.shape[1]
    pairs = kept.reshape(blocks, 32, 2, width)
    kinds = jnp.arange(6, dtype=jnp.int32)[:, None, None]
    table_first = jnp.array([0, 0, 0, 1, 1, 2], dtype=jnp.int32)[:, None, None]
    table_second = jnp.array([1, 2, 3, 2, 3, 3], dtype=jnp.int32)[:, None, None]
    match = (codes[None, :, :] == kinds).astype(jnp.int32)
    first = jnp.sum(table_first * match, axis=0)
    second = jnp.sum(table_second * match, axis=0)
    position = lax.broadcasted_iota(jnp.int32, (1, 1, 4, 1), 2)
    zero = jnp.zeros((), kept.dtype)
    dense = jnp.where(position == first[:, None, None, :], pairs[:, :, 0:1, :], zero)
    dense = dense + jnp.where(position == second[:, None, None, :], pairs[:, :, 1:2, :], zero)
    return dense.reshape(blocks * 128, width)


def on_device(tokens, gate_kept, up_kept, gate_keep, up_keep, down_weight):
    gate_dense = expand(gate_kept, gate_keep)
    up_dense = expand(up_kept, up_keep)
    rows_width, local_hidden = gate_dense.shape
    groups = lax.axis_size("section")
    share_width = local_hidden // groups
    stacked = jnp.stack(
        (
            gate_dense.reshape(rows_width, groups, share_width),
            up_dense.reshape(rows_width, groups, share_width),
        ),
        axis=2,
    ).reshape(rows_width, 2 * local_hidden)
    partial_sums = jnp.dot(
        lax.all_gather(tokens, "wide", axis=0, tiled=True),
        stacked,
        preferred_element_type=jnp.float32,
    )
    count = partial_sums.shape[0]
    share = lax.psum_scatter(partial_sums, "section", scatter_dimension=1, tiled=True)
    shaped = share.reshape(count, 2, share_width)
    quarter = (jax.nn.silu(shaped[:, 0]) * shaped[:, 1]).astype(jnp.bfloat16)
    hidden = lax.all_gather(quarter, "section", axis=1, tiled=True)
    next_input = lax.psum_scatter(
        jnp.dot(hidden, down_weight, preferred_element_type=jnp.float32),
        "wide",
        scatter_dimension=0,
        tiled=True,
    ).astype(jnp.bfloat16)
    gathered = lax.all_gather(next_input, "wide", axis=0, tiled=True)
    section_width = gathered.shape[1]
    column_width = section_width * groups // lax.axis_size("wide")
    start_column = lax.axis_index("wide") * column_width
    root = start_column // section_width
    offset = start_column % section_width
    selected = lax.dynamic_slice_in_dim(gathered, offset, column_width, 1)
    columns = from_root(selected, "section", root)
    gram = lax.dot_general(
        gathered, columns, (((0,), (0,)), ((), ())), preferred_element_type=jnp.float32
    )
    gram = gram * (1.0 / math.sqrt(gathered.shape[0]))
    return (next_input, gram)


def solution(mesh):
    return jax.shard_map(
        on_device,
        mesh=mesh,
        in_specs=(
            P("wide", "section"),
            P("section", "wide"),
            P("section", "wide"),
            P("section", "wide"),
            P("section", "wide"),
            P("wide", "section"),
        ),
        out_specs=(P("wide", "section"), P("section", "wide")),
        check_vma=False,
    )
```

profile of v0, /device:TPU:0, one launch (start us, length us, event | category | flops | bytes accessed | tf_op | source)
XLA Modules:
  0.0 791.1 jit_solution(11238831395752129062)
XLA Ops:
  7.2 0.0 reduce-scatter.3.cloned.1.call-start
  7.2 27.0 %reshape.137 = bf16[32,32,2,4096]{3,2,1,0:T(2,128)(2,1)} reshape(bf16[2048,4096]{1,0:T(8,128)(2,1)} %param.12) | data formatting | bytes 33554432 | tf_op jit(solution)/shard_map/reshape | solution.py:17
  34.2 0.0 copy-start
  34.2 0.0 copy-start.1
  34.2 0.0 copy-start.4
  34.2 0.0 copy-start.5
  34.2 36.6 %fusion.2 = (bf16[32,32,1,4096]{3,2,1,0:T(2,128)(2,1)S(1)}, bf16[32,32,1,4096]{3,2,1,0:T(2,128)(2,1)}) fusion(bf16[32,32,2,4096]{3,2,1,0:T(2,128)(2,1)} %reshape.137), kind=kLoop, calls=%fused_computation.24 | loop fusion | bytes 33554432 | tf_op jit(solution)/shard_map/slice | solution.py:26
  70.8 0.0 copy-done
  70.9 0.0 copy-done.1
  70.9 0.0 copy-done.4
  70.9 0.0 copy-done.5
  70.9 1.1 select_reduce_fusion.1
  72.0 1.3 iota_compare_fusion.2
  73.3 25.8 %copy_bitcast_fusion = (bf16[32,32,4096]{2,1,0:T(8,128)(2,1)}, bf16[32,32,4096]{2,1,0:T(8,128)(2,1)}) fusion(bf16[32,32,1,4096]{3,2,1,0:T(2,128)(2,1)} %get-tuple-element.11, bf16[32,32,1,4096]{3,2,1,0:T(2,128)(2,1)S(1)} %get-tuple-element.10), kind=kLoop, calls=%fused_computation.5 | loop fusion | bytes 33554432
  99.1 34.5 %select_add_fusion = bf16[32,32,4,4096]{3,2,1,0:T(4,128)(2,1)} fusion(pred[32,4,4096]{2,1,0:T(4,128)(4,1)S(1)} %get-tuple-element.14, pred[32,4,4096]{2,1,0:T(4,128)(4,1)S(1)} %get-tuple-element.15, bf16[32,32,4096]{2,1,0:T(8,128)(2,1)} %get-tuple-element.18, bf16[32,32,4096]{2,1,0:T(8,128)(2,1)} %get-tuple-element.19), kind=kLoop, calls=%fused_computation.1 | loop fusion | flops 50331648 | bytes 51380224 | tf_op jit(solution)/shard_map/add | solution.py:27
  133.5 54.8 %add.47 = bf16[4096,4,1,1024]{3,1,0,2:T(4,128)(2,1)} reshape(bf16[32,32,4,4096]{3,2,1,0:T(4,128)(2,1)} %select_add_fusion) | data formatting | bytes 67108864 | tf_op jit(solution)/shard_map/add | solution.py:27
  188.3 27.0 %reshape.136 = bf16[32,32,2,4096]{3,2,1,0:T(2,128)(2,1)} reshape(bf16[2048,4096]{1,0:T(8,128)(2,1)} %param.11) | data formatting | bytes 33554432 | tf_op jit(solution)/shard_map/reshape | solution.py:17
  215.3 36.6 %fusion.1 = (bf16[32,32,1,4096]{3,2,1,0:T(2,128)(2,1)S(1)}, bf16[32,32,1,4096]{3,2,1,0:T(2,128)(2,1)}) fusion(bf16[32,32,2,4096]{3,2,1,0:T(2,128)(2,1)} %reshape.136), kind=kLoop, calls=%fused_computation.23 | loop fusion | bytes 33554432 | tf_op jit(solution)/shard_map/slice | solution.py:26
  251.9 1.4 iota_compare_fusion.4
  253.3 25.8 %copy_bitcast_fusion.2 = (bf16[32,32,4096]{2,1,0:T(8,128)(2,1)}, bf16[32,32,4096]{2,1,0:T(8,128)(2,1)}) fusion(bf16[32,32,1,4096]{3,2,1,0:T(2,128)(2,1)} %get-tuple-element.9, bf16[32,32,1,4096]{3,2,1,0:T(2,128)(2,1)S(1)} %get-tuple-element.8), kind=kLoop, calls=%fused_computation.7 | loop fusion | bytes 33554432
  279.1 34.5 %select_add_fusion.1 = bf16[32,32,4,4096]{3,2,1,0:T(4,128)(2,1)} fusion(pred[32,4,4096]{2,1,0:T(4,128)(4,1)S(1)} %get-tuple-element.16, pred[32,4,4096]{2,1,0:T(4,128)(4,1)S(1)} %get-tuple-element.17, bf16[32,32,4096]{2,1,0:T(8,128)(2,1)} %get-tuple-element.20, bf16[32,32,4096]{2,1,0:T(8,128)(2,1)} %get-tuple-element.21), kind=kLoop, calls=%fused_computation.2 | loop fusion | flops 50331648 | bytes 51380224 | tf_op jit(solution)/shard_map/add | solution.py:27
  313.6 54.8 %add.45 = bf16[4096,4,1,1024]{3,1,0,2:T(4,128)(2,1)} reshape(bf16[32,32,4,4096]{3,2,1,0:T(4,128)(2,1)} %select_add_fusion.1) | data formatting | bytes 67108864 | tf_op jit(solution)/shard_map/add | solution.py:27
  368.4 54.0 %pad_maximum_fusion = bf16[4096,4,2,1024]{3,1,0,2:T(4,128)(2,1)} fusion(bf16[4096,4,1,1024]{3,1,0,2:T(4,128)(2,1)} %add.47, bf16[4096,4,1,1024]{3,1,0,2:T(4,128)(2,1)} %add.45), kind=kLoop, calls=%fused_computation | loop fusion | flops 33554432 | bytes 134217728 | tf_op jit(solution)/shard_map/stack | solution.py:37
  422.4 0.0 copy-start.3
  422.4 100.5 %copy.20 = bf16[4096,4,2,1024]{0,3,2,1:T(8,128)(2,1)} copy(bf16[4096,4,2,1024]{3,1,0,2:T(4,128)(2,1)} %pad_maximum_fusion) | data formatting | bytes 134217728 | tf_op jit(solution)/shard_map/stack | solution.py:37
  522.9 0.0 copy-done.3
  522.9 33.0 %all_gather.9 = bf16[64,4096]{1,0:T(8,128)(2,1)S(1)} all-gather(bf16[8,4096]{1,0:T(8,128)(2,1)S(1)} %copy-done.3), channel_id=1, replica_groups=mesh['wide'=8,'section'=4] {'wide'}, dimensions={0}, use_global_device_ids=true | all-gather | bytes 589824 | tf_op jit(solution)/shard_map/all_gather | solution.py:45
  555.9 28.6 %convolution_bitcast_fusion = f32[64,8192]{1,0:T(8,128)} fusion(bf16[4096,8192]{0,1:T(8,128)(2,1)} %bitcast, bf16[64,4096]{1,0:T(8,128)(2,1)S(1)} %all_gather.9), kind=kOutput, calls=%fused_computation.4 | convolution fusion | flops 4294967296 | bytes 69730304 | tf_op jit(solution)/shard_map/dot_general | solution.py:44
  584.6 0.0 reduce-scatter.3.cloned.1.call-update
  584.6 0.0 reduce-scatter.5.cloned.1.call-start
  584.6 32.4 %reduce-scatter.3.cloned.1.call-done = f32[64,2048]{1,0:T(8,128)} async-done(((f32[64,8192]{1,0:T(8,128)}), f32[64,2048]{1,0:T(8,128)}) %reduce-scatter.3.cloned.1.call-update) | async-done | bytes 524304 | tf_op jit(solution)/shard_map/reduce_scatter | solution.py:50
  617.0 1.5 reshape.139
  618.5 0.4 fusion.3
  618.9 0.1 fusion
  619.0 6.6 all_gather.10
  625.6 14.5 %fusion.4 = f32[64,4096]{1,0:T(8,128)} fusion(bf16[64,4096]{1,0:T(8,128)(2,1)S(1)} %all_gather.10, bf16[4096,4096]{1,0:T(8,128)(2,1)} %param.15), kind=kOutput, calls=%fused_computation.26 | convolution fusion | flops 2147483648 | bytes 35127296 | tf_op jit(solution)/shard_map/dot_general | solution.py:55
  640.2 0.0 reduce-scatter.5.cloned.1.call-update
  640.2 0.0 all-reduce.2.cloned.1.call-start
  640.3 64.8 %reduce-scatter.5.cloned.1.call-done = f32[8,4096]{1,0:T(8,128)} async-done(((f32[64,4096]{1,0:T(8,128)}), f32[8,4096]{1,0:T(8,128)}) %reduce-scatter.5.cloned.1.call-update) | async-done | bytes 131088 | tf_op jit(solution)/shard_map/reduce_scatter | solution.py:54
  705.1 0.9 convert_element_type.11
  706.0 0.0 copy-start.2
  706.0 31.5 %all_gather.11 = bf16[64,4096]{1,0:T(8,128)(2,1)S(1)} all-gather(bf16[8,4096]{1,0:T(8,128)(2,1)S(1)} %convert_element_type.11), channel_id=1, replica_groups=mesh['wide'=8,'section'=4] {'wide'}, dimensions={0}, use_global_device_ids=true | all-gather | bytes 589824 | tf_op jit(solution)/shard_map/all_gather | solution.py:60
  737.5 0.7 dynamic-slice_select_fusion
  738.3 0.0 all-reduce.2.cloned.1.call-update
  738.3 31.2 %all-reduce.2.cloned.1.call-done = bf16[64,2048]{1,0:T(8,128)(2,1)} async-done(((bf16[64,2048]{1,0:T(8,128)(2,1)}), bf16[64,2048]{1,0:T(8,128)(2,1)}) %all-reduce.2.cloned.1.call-update) | async-done | bytes 262160 | tf_op jit(solution)/shard_map/psum | solution.py:11
  769.5 15.0 %broadcast_multiply_fusion = f32[4096,2048]{1,0:T(8,128)} fusion(bf16[64,4096]{1,0:T(8,128)(2,1)S(1)} %all_gather.11, bf16[64,2048]{1,0:T(8,128)(2,1)} %all-reduce.2.cloned.1.call-done), kind=kOutput, calls=%fused_computation.3 | convolution fusion | flops 1082130432 | bytes 34340864 | tf_op jit(solution)/shard_map/dot_general | solution.py:68
  784.5 0.0 copy-done.2
Async XLA Ops:
  7.2 609.9 %reduce-scatter.3.cloned.1.call-start = ((), (), s32[]{:S(2)}) async-start(), calls=%async_computation.2 | async-start | bytes 2621440 | tf_op jit(solution)/shard_map/reduce_scatter | solution.py:50
  34.2 36.6 %copy-start = (s32[32,4096]{1,0:T(8,128)S(1)}, s32[32,4096]{1,0:T(8,128)}, u32[]{:S(2)}) copy-start(s32[32,4096]{1,0:T(8,128)} %param.14) | copy-start | bytes 1572868
  34.2 36.7 %copy-start.1 = (s32[32,4096]{1,0:T(8,128)S(1)}, s32[32,4096]{1,0:T(8,128)}, u32[]{:S(2)}) copy-start(s32[32,4096]{1,0:T(8,128)} %param.13) | copy-start | bytes 1572868
  34.2 36.7 %copy-start.4 = (s32[6]{0:T(128)S(1)}, s32[6]{0:T(128)}, u32[]{:S(2)}) copy-start(s32[6]{0:T(128)} %constant.54.clone) | copy-start | bytes 76
  34.2 36.7 %copy-start.5 = (s32[6]{0:T(128)S(1)}, s32[6]{0:T(128)}, u32[]{:S(2)}) copy-start(s32[6]{0:T(128)} %constant.55.clone) | copy-start | bytes 76
  422.4 100.5 %copy-start.3 = (bf16[8,4096]{1,0:T(8,128)(2,1)S(1)}, bf16[8,4096]{1,0:T(8,128)(2,1)}, u32[]{:S(2)}) copy-start(bf16[8,4096]{1,0:T(8,128)(2,1)} %param.10) | copy-start | bytes 196612
  584.6 120.5 %reduce-scatter.5.cloned.1.call-start = ((), (), s32[]{:S(2)}) async-start(), calls=%async_computation.3 | async-start | bytes 1179648 | tf_op jit(solution)/shard_map/reduce_scatter | solution.py:54
  640.2 129.3 %all-reduce.2.cloned.1.call-start = ((), (), s32[]{:S(2)}) async-start(), calls=%async_computation.4 | async-start | bytes 524288 | tf_op jit(solution)/shard_map/psum | solution.py:11
  706.0 78.5 %copy-start.2 = (bf16[8,4096]{1,0:T(8,128)(2,1)}, bf16[8,4096]{1,0:T(8,128)(2,1)S(1)}, u32[]{:S(2)}) copy-start(bf16[8,4096]{1,0:T(8,128)(2,1)S(1)} %convert_element_type.11) | copy-start | bytes 196612
Sparse Core Ops, SparseCore 0:
  584.7 32.2 reduce-scatter.2
  640.3 64.7 reduce-scatter.4
  738.4 31.0 all-reduce.1
where the time goes:
time: 798 us; the launch traced here: 791 us
  local copies, waits for them, and re-layouts  391 us (49%)
  other arithmetic  129 us (16%)
  waiting for transfers between devices  128 us (16%)
  blocking collectives  71.2 us (9%)
  matrix products  58.1 us (7%)
  between operations  13.9 us (2%)
    add x2, local copies, waits for them, and re-layouts, expand(): dense + jnp.where(position == second[:, None, None, :], pairs[:, :, 1:2,...  110 us
    another operation x1, local copies, waits for them, and re-layouts, on_device(): jnp.stack((gate_dense.reshape(rows_width, groups, share_width), up_dense....  100 us
    slice x2, local copies, waits for them, and re-layouts, expand(): pairs[:, :, 0:1, :]  73.2 us
    add x2, other arithmetic, expand(): dense + jnp.where(position == second[:, None, None, :], pairs[:, :, 1:2,...  68.9 us
    reduce_scatter x1, waiting for transfers between devices, on_device(): lax.psum_scatter(jnp.dot(hidden, down_weight, preferred_element_type=jnp....  64.8 us
    another operation x1, other arithmetic, on_device(): jnp.stack((gate_dense.reshape(rows_width, groups, share_width), up_dense....  54 us
    reshape x2, local copies, waits for them, and re-layouts, expand(): pairs = kept.reshape(blocks, 32, 2, width)  54 us
    unnamed x14, local copies, waits for them, and re-layouts  51.6 us
  transfers between devices with their start and end apart: 3, of which 3 were waited for; matrix products, arithmetic and copies ran while one was open for 0% of the time, Pallas kernels for 0%

commit v1 on v0

v1 whole, which is shorter than its diff:
```python
import functools
import math

import jax
import jax.numpy as jnp
from jax import lax
from jax.experimental import pallas as pl
from jax.experimental.pallas import tpu as pltpu
from jax.sharding import PartitionSpec as P

F32, BF16 = jnp.float32, jnp.bfloat16
ROWS, GROUP = 128, 4
MIB = 1 << 20


def tile(limit, width):
    return limit if width % limit == 0 else width


def call(kernel, name, grid, scalars, inputs, outputs, scratch=(), cost=(0, 0), vmem=48):
    arrays, in_specs = zip(*inputs)
    shapes, out_specs = zip(*outputs)
    return pl.pallas_call(
        kernel,
        name=name,
        grid_spec=pltpu.PrefetchScalarGridSpec(
            num_scalar_prefetch=1,
            grid=grid,
            in_specs=list(in_specs),
            out_specs=list(out_specs),
            scratch_shapes=list(scratch),
        ),
        out_shape=list(shapes),
        cost_estimate=pl.CostEstimate(flops=cost[0], bytes_accessed=cost[1], transcendentals=0),
        compiler_params=pltpu.CompilerParams(vmem_limit_bytes=vmem * MIB),
    )(scalars, *arrays)


def whole(shape):
    return pl.BlockSpec(shape, lambda *_: (0,) * len(shape))


def arrange_kernel(near, where, *refs):
    own, other, out = refs[:near], refs[near:2 * near], refs[2 * near]
    deep = 2 * ROWS
    row = lax.broadcasted_iota(jnp.int32, (deep, 3 * ROWS), 0)
    column = lax.broadcasted_iota(jnp.int32, (deep, 3 * ROWS), 1)
    kind, lane = column // ROWS, column % ROWS
    block, group, second = lane // (ROWS // 2), (lane % (ROWS // 2)) // 2, lane % 2
    place = jnp.where(second == 0, kind, 3 - kind)
    mix = jnp.where(row == block * ROWS + group * GROUP + place, 1.0, 0.0).astype(BF16)
    chunks = own[0].shape[1] // deep
    first = where[2] == 0
    for k in range(near):
        a, b = own[k][...].astype(F32), other[k][...].astype(F32)
        both = jnp.concatenate((jnp.where(first, a, b), jnp.where(first, b, a)), axis=0).astype(BF16)
        rows = both.shape[0]
        flat = jnp.concatenate([both[:, deep * i:deep * (i + 1)] for i in range(chunks)], axis=0)
        mixed = jnp.dot(flat, mix, preferred_element_type=F32).astype(BF16)
        at = pl.multiple_of((where[1] ^ k) * rows, rows)
        for i in range(chunks):
            for n in range(3):
                out[n, pl.ds(at, rows), ROWS * i:ROWS * (i + 1)] = mixed[rows * i:rows * (i + 1), ROWS * n:ROWS * (n + 1)]


def share_kernel(where, tokens, gate, up, gate_code, up_code, out, place):
    depth, width = gate.shape
    blocks = gate_code.shape[0]
    kept = depth // blocks
    many = 4 if blocks % 4 == 0 else 1
    even = lax.broadcasted_iota(jnp.int32, (16, width), 0) % 2 == 0
    for side, (values, codes) in enumerate(((gate, gate_code), (up, up_code))):
        code = codes[...]
        place[0] = jnp.where(code < 3, 0.0, jnp.where(code < 5, 1.0, 2.0))
        place[1] = jnp.where(code == 0, 2.0, jnp.where((code == 1) | (code == 3), 1.0, 0.0))
        total = jnp.zeros(out.shape[1:], F32)
        for q in range(blocks // many):
            parts = ([], [], [])
            for k in range(many * q, many * (q + 1)):
                first = jnp.broadcast_to(place[0, pl.ds(k, 1), :], (16, width))
                second = jnp.broadcast_to(place[1, pl.ds(k, 1), :], (16, width))
                kind = jnp.where(even, first, second)
                value = values[kept * k:kept * (k + 1), :]
                for n in range(3):
                    mask = jnp.where(kind == n, 1.0, 0.0).astype(BF16)
                    parts[n].append(value * jnp.concatenate([mask] * (kept // 16), axis=0))
            span = many * kept
            for n in range(3):
                part = jnp.concatenate(parts[n], axis=0)
                total = total + jnp.dot(tokens[n, :, span * q:span * (q + 1)], part, preferred_element_type=F32)
        out[side] = total


def down_kernel(count, adds, where, *refs):
    hidden, weights, rest = refs[:count], refs[count:2 * count], refs[2 * count:]
    total = rest[0][...] if adds else None
    for left, right in zip(hidden, weights):
        product = jnp.dot(left[...], right[...], preferred_element_type=F32)
        total = product if total is None else total + product
    rest[-1][...] = total.astype(rest[-1].dtype)


def split_kernel(where, mine, theirs, *outs):
    rows = outs[0].shape[0]
    for k, out in enumerate(outs):
        at = pl.ds(pl.multiple_of((where[1] ^ k) * rows, rows), rows)
        out[...] = (mine[at, :] + theirs[at, :].astype(F32)).astype(out.dtype)


def finish_kernel(where, *refs):
    total = refs[0][...]
    for ref in refs[1:-1]:
        total = total + ref[...].astype(F32)
    refs[-1][...] = total.astype(BF16)


def join_kernel(where, *refs):
    out = refs[-1]
    rows = refs[0].shape[0]
    for k, ref in enumerate(refs[:-1]):
        out[pl.ds(pl.multiple_of((where[1] ^ k) * rows, rows), rows), :] = ref[...]


def gram_kernel(scale, per, where, own, other, columns, out, tokens_out):
    step = pl.program_id(0)
    rows = out.shape[0]
    half = own.shape[1] // rows
    at = pl.ds(pl.multiple_of((step % half) * rows, rows), rows)
    block = jnp.where(step < half, own[:, at], other[:, at])
    product = lax.dot_general(block, columns[...], (((0,), (0,)), ((), ())), preferred_element_type=F32)
    out[...] = product * scale

    @pl.when(step == 0)
    def _():
        count = tokens_out.shape[0]
        pick = pl.ds(pl.multiple_of(where[1] * 2 * count, 2 * count), 2 * count)
        width = columns.shape[1]
        for index, ref in enumerate((own, other)):
            both = ref[pick, :].astype(F32)
            lines = jnp.where(where[2] == 0, both[:count], both[count:]).astype(BF16)
            for j in range(per):
                side = where[2] ^ index
                to = pl.ds(pl.multiple_of((2 * j + side) * width, width), width)
                tokens_out[:, to] = lines[:, width * j:width * (j + 1)]


def on_device(tokens, gate_kept, up_kept, gate_keep, up_keep, down_weight):
    wide, groups = lax.axis_size("wide"), lax.axis_size("section")
    deep, across = wide // 2, groups // 2
    w, s = lax.axis_index("wide"), lax.axis_index("section")
    z, y, x, c = w // 2, w % 2, s // 2, s % 2
    near = deep <= 4
    kept_rows, local_hidden = gate_kept.shape
    blocks = gate_keep.shape[0]
    own_tokens, section_width = tokens.shape
    count = own_tokens * wide
    share = local_hidden // groups
    half = section_width // 2
    column_width = section_width * groups // wide
    runs = half // column_width

    def scalars(*more):
        return jnp.stack([jnp.asarray(v, jnp.int32) for v in (w, z, y) + more])

    base = scalars()
    pairs = [(i, i ^ 1) for i in range(wide)]
    swap_y = lambda v: lax.ppermute(v, "wide", pairs)
    swap_core = lambda v: lax.ppermute(v, "section", [(i, i ^ 1) for i in range(groups)])
    turn_x = lambda v, j: lax.ppermute(v, "section", [(i, (i + 2 * j) % groups) for i in range(groups)])
    hop_z = lambda v, k: lax.ppermute(v, "wide", [(i, i ^ (2 * k)) for i in range(wide)])
    lines = [[2 * i + e for i in range(deep)] for e in range(2)]

    if near:
        own = [tokens] + [hop_z(tokens, k) for k in range(1, deep)]
        stacked = swap_y(jnp.concatenate(own, axis=0))
        other = [stacked[own_tokens * k:own_tokens * (k + 1)] for k in range(deep)]
        order = base
    else:
        gathered = lax.all_gather(tokens, "wide", axis=0, tiled=True).reshape(deep, 2, own_tokens, section_width)
        own = [gathered[k, 0] for k in range(deep)]
        other = [gathered[k, 1] for k in range(deep)]
        order = jnp.zeros_like(base)
    paired = jax.ShapeDtypeStruct((3, count, section_width // 2), BF16)
    (arranged,) = call(
        functools.partial(arrange_kernel, deep), "arrange", (1,), order,
        [(v, whole(v.shape)) for v in own + other], [(paired, whole(paired.shape))],
    )

    width = tile(512, share)
    steps = share // width

    def partial_share(to_x, to_c):
        q = to_x * 2 + to_c
        piece = lambda rows: pl.BlockSpec((rows, width), lambda j, where: (0, where[3] * steps + j))
        (out,) = call(
            share_kernel, "share", (steps,), scalars(q),
            [(arranged, whole(arranged.shape)), (gate_kept, piece(kept_rows)), (up_kept, piece(kept_rows)),
             (gate_keep, piece(blocks)), (up_keep, piece(blocks))],
            [(jax.ShapeDtypeStruct((2, count, share), F32), pl.BlockSpec((2, count, width), lambda j, where: (0, 0, j)))],
            [pltpu.VMEM((2, blocks, width), F32)],
            cost=(12 * count * kept_rows * share, 4 * kept_rows * share),
        )
        return out

    arrived = []
    for j in range(1, across + 1):
        to_x = (x + j) % across
        sent = swap_core(partial_share(to_x, c ^ 1))
        mine = partial_share(to_x, c)
        if j < across:
            arrived.append(turn_x(mine + sent, j))
    total = mine + sent
    for value in arrived:
        total = total + value
    quarter = (jax.nn.silu(total[0]) * total[1]).astype(BF16)

    block = tile(512, column_width)
    ratio = column_width // block

    def down(hidden, order, adds, side, dtype):
        place = scalars(*order, y if side is None else (y ^ side))
        n = len(hidden)
        if side is None:
            column = lambda j, where: j
        else:
            column = lambda j, where: ((j // ratio) * 2 + where[3 + n]) * ratio + j % ratio
        size = section_width if side is None else half
        inputs = [(v, whole(v.shape)) for v in hidden]
        inputs += [(down_weight, pl.BlockSpec((share, block), functools.partial(lambda i, j, where: (where[3 + i], column(j, where)), i))) for i in range(n)]
        if adds is not None:
            inputs.append((adds, pl.BlockSpec((count, block), lambda j, where: (0, column(j, where)))))
        (out,) = call(
            functools.partial(down_kernel, n, adds is not None), "down", (size // block,), place, inputs,
            [(jax.ShapeDtypeStruct((count, size), dtype), pl.BlockSpec((count, block), lambda j, where: (0, j)))],
            cost=(2 * count * share * size * n, 2 * share * size * n),
        )
        return out

    beside = swap_core(quarter)
    far = [turn_x(quarter, j) for j in range(1, across)]
    near_sum = down([quarter, beside], [x * 2 + c, x * 2 + (c ^ 1)], None, None, F32)
    more, more_order = [], []
    for j in range(1, across):
        from_x = (x - j) % across
        more += [far[j - 1], swap_core(far[j - 1])]
        more_order += [from_x * 2 + c, from_x * 2 + (c ^ 1)]
    sent = swap_y(down(more, more_order, near_sum, 1, BF16))
    mine = down(more, more_order, near_sum, 0, F32)

    rows = count // deep
    if near:
        piece = lambda dtype: (jax.ShapeDtypeStruct((rows, half), dtype), whole((rows, half)))
        parts = call(
            split_kernel, "split", (1,), base, [(mine, whole(mine.shape)), (sent, whole(sent.shape))],
            [piece(F32)] + [piece(BF16)] * (deep - 1),
        )
        parts = [parts[0]] + [hop_z(v, k) for k, v in enumerate(parts) if k]
        (final,) = call(finish_kernel, "finish", (1,), base, [(v, whole(v.shape)) for v in parts], [piece(BF16)])
        pieces = [final] + [hop_z(final, k) for k in range(1, deep)]
        joined = jax.ShapeDtypeStruct((count, half), BF16)
        (ours,) = call(join_kernel, "join", (1,), base, [(v, whole(v.shape)) for v in pieces], [(joined, whole(joined.shape))])
    else:
        both = (mine + sent.astype(F32)).astype(BF16)
        parts = lax.all_to_all(both, "wide", 0, 0, tiled=True, axis_index_groups=lines)
        final = jnp.sum(parts.reshape(deep, rows, half).astype(F32), axis=0).astype(BF16)
        ours = lax.all_gather(final, "wide", axis=0, tiled=True, axis_index_groups=lines)
    theirs = swap_y(ours)

    per = wide // groups
    root = [i // per for i in range(wide)]
    at_root = w // per
    held = lax.dynamic_slice_in_dim(ours, ((w % per) // 2) * column_width, column_width, 1)
    held = jnp.where(s == at_root, held, 0).astype(BF16)
    everywhere = ("wide", "section")
    same_core = held
    for j in range(1, across):
        step = [(i * groups + root[i], i * groups + (root[i] + 2 * j) % groups) for i in range(wide)]
        same_core = same_core + lax.ppermute(held, everywhere, step)
    columns = same_core + jnp.where((s ^ at_root) % 2 == 0, 0, swap_core(same_core)).astype(BF16)

    line = tile(512, column_width)
    each = column_width // line

    def natural(i, where):
        side, j = i // (half // line), i % (half // line)
        return ((j // each) * 2 + (where[2] ^ side)) * each + j % each

    gram, next_input = call(
        functools.partial(gram_kernel, 1.0 / math.sqrt(count), runs), "gram", (section_width // line,), base,
        [(ours, whole(ours.shape)), (theirs, whole(theirs.shape)), (columns, whole(columns.shape))],
        [(jax.ShapeDtypeStruct((section_width, column_width), F32), pl.BlockSpec((line, column_width), lambda i, where: (natural(i, where), 0))),
         (jax.ShapeDtypeStruct((own_tokens, section_width), BF16), whole((own_tokens, section_width)))],
        cost=(2 * count * section_width * column_width, 4 * section_width * column_width),
    )
    return (next_input, gram)


def solution(mesh):
    return jax.shard_map(
        on_device,
        mesh=mesh,
        in_specs=(
            P("wide", "section"),
            P("section", "wide"),
            P("section", "wide"),
            P("section", "wide"),
            P("section", "wide"),
            P("wide", "section"),
        ),
        out_specs=(P("wide", "section"), P("section", "wide")),
        check_vma=False,
    )
```

time: 798 us -> 139 us (0.17)
  local copies, waits for them, and re-layouts: 391 us -> 3.18 us
  other arithmetic: 129 us -> 1.42 us
  waiting for transfers between devices: 128 us -> 39 us
  blocking collectives: 71.2 us -> 0 us
  Pallas kernels: 0 us -> 67.1 us
  matrix products: 58.1 us -> 0 us
  starting transfers between devices: 0.12 us -> 27 us
  between operations: 13.9 us -> 0.86 us
    add x2 -> x0, local copies, waits for them, and re-layouts: 110 us -> none  [expand(): dense + jnp.where(position == second[:, None, None, :], pairs[:, :, 1:2,...]
    another operation x1 -> x3, local copies, waits for them, and re-layouts: 100 us -> 0.25 us  [scalars(): return jnp.stack([jnp.asarray(v, jnp.int32) for v in (w, z, y) + more])]
    reduce_scatter x2 -> x0, waiting for transfers between devices: 97.2 us -> none  [the longest x1 64.8 us: on_device(): lax.psum_scatter(jnp.dot(hidden, down_weight, preferred_element_type=jnp....]
    slice x3 -> x1, local copies, waits for them, and re-layouts: 73.7 us -> 0.02 us  [on_device(): other = [stacked[own_tokens * k:own_tokens * (k + 1)] for k in range(deep)]]
    all_gather x3 -> x0, blocking collectives: 71.2 us -> none  [the longest x1 33 us: on_device(): lax.all_gather(tokens, 'wide', axis=0, tiled=True)]
    add x2 -> x4, other arithmetic: 68.9 us -> 0.23 us  [the longest x1 0.11 us: on_device(): total = total + value]
    pallas_call x0 -> x12, Pallas kernels: none -> 67.1 us  [call(): pl.pallas_call(kernel, name=name, grid_spec=pltpu.PrefetchScalarGridSpec(...]
    dot_general x3 -> x0, matrix products: 58.1 us -> none  [the longest x1 28.6 us: on_device(): jnp.dot(lax.all_gather(tokens, 'wide', axis=0, tiled=True), stacked, pref...]
  transfers between devices with their start and end apart: 3 -> 20, of which waited for: 3 -> 13; matrix products, arithmetic and copies ran while one was open for 0% -> 0% of each run, Pallas kernels for 0% -> 28%
where the time goes in v1:
time: 139 us
  Pallas kernels  67.1 us (48%)
  waiting for transfers between devices  39 us (28%)
  starting transfers between devices  27 us (19%)
  local copies, waits for them, and re-layouts  3.18 us (2%)
  other arithmetic  1.42 us (1%)
    pallas_call x12, Pallas kernels, call(): pl.pallas_call(kernel, name=name, grid_spec=pltpu.PrefetchScalarGridSpec(...  67.1 us
    ppermute x3, waiting for transfers between devices, on_device(): swap_y = lambda v: lax.ppermute(v, 'wide', pairs)  14.7 us
    ppermute x9, starting transfers between devices, on_device(): lax.ppermute(v, 'wide', [(i, i ^ 2 * k) for i in range(wide)])  14.7 us
    ppermute x9, waiting for transfers between devices, on_device(): lax.ppermute(v, 'wide', [(i, i ^ 2 * k) for i in range(wide)])  12.4 us
    ppermute x2, waiting for transfers between devices, on_device(): lax.ppermute(v, 'section', [(i, (i + 2 * j) % groups) for i in range(grou...  7.98 us
    ppermute x3, starting transfers between devices, on_device(): swap_y = lambda v: lax.ppermute(v, 'wide', pairs)  4.87 us
    ppermute x1, waiting for transfers between devices, on_device(): same_core = same_core + lax.ppermute(held, everywhere, step)  3.86 us
    ppermute x1, starting transfers between devices, on_device(): same_core = same_core + lax.ppermute(held, everywhere, step)  3.41 us
  transfers between devices with their start and end apart: 20, of which 13 were waited for; matrix products, arithmetic and copies ran while one was open for 0% of the time, Pallas kernels for 28%

profile of v1, /device:TPU:0, one launch (start us, length us, event | category | flops | bytes accessed | tf_op | source)
XLA Modules:
  0.0 138.6 jit_solution(6645378591793233801)
XLA Ops:
  0.6 5.1 %collective-permute-start.2 = (bf16[8,4096]{1,0:T(8,128)(2,1)}, bf16[8,4096]{1,0:T(8,128)(2,1)S(1)}, u32[]{:S(2)}, u32[]{:S(2)}) collective-permute-start(bf16[8,4096]{1,0:T(8,128)(2,1)} %refs_0_.1), channel_id=1, source_target_pairs={{0,24},{4,28},{8,16},{12,20},{16,8},{20,12},{24,0},{28,4},{1,25},{... | collective-permute-start | bytes 196616 | tf_op jit(solution)/shard_map/ppermute | solution.py:170
  5.8 0.0 collective-permute-start.1
  5.8 0.6 collective-permute-start
  6.4 0.1 pad_add_fusion.3
  6.5 2.1 %collective-permute-done.2.refs_3_ = bf16[8,4096]{1,0:T(8,128)(2,1)S(1)} collective-permute-done((bf16[8,4096]{1,0:T(8,128)(2,1)}, bf16[8,4096]{1,0:T(8,128)(2,1)S(1)}, u32[]{:S(2)}, u32[]{:S(2)}) %collective-permute-start.2) | collective-permute-done | bytes 65568 | tf_op jit(solution)/shard_map/ppermute | solution.py:170
  8.6 3.0 %collective-permute-done.1.refs_2_ = bf16[8,4096]{1,0:T(8,128)(2,1)S(1)} collective-permute-done((bf16[8,4096]{1,0:T(8,128)(2,1)}, bf16[8,4096]{1,0:T(8,128)(2,1)S(1)}, u32[]{:S(2)}, u32[]{:S(2)}) %collective-permute-start.1) | collective-permute-done | bytes 65568 | tf_op jit(solution)/shard_map/ppermute | solution.py:170
  11.6 0.9 pad_maximum_fusion
  12.5 1.6 %collective-permute-start.3 = (bf16[32,4096]{1,0:T(8,128)(2,1)S(1)}, bf16[32,4096]{1,0:T(8,128)(2,1)S(1)}, u32[]{:S(2)}, u32[]{:S(2)}) collective-permute-start(bf16[32,4096]{1,0:T(8,128)(2,1)S(1)} %pad_maximum_fusion), channel_id=1, source_target_pairs={{0,4},{4,0},{8,12},{12,8},{16,20},{20,16},{24,28},{28,24},{1,5},{5... | collective-permute-start | bytes 786440 | tf_op jit(solution)/shard_map/ppermute | solution.py:167
  14.0 0.1 pad_add_fusion.where
  14.1 0.1 pad_add_fusion.1
  14.2 6.2 %collective-permute-done.3 = bf16[32,4096]{1,0:T(8,128)(2,1)S(1)} collective-permute-done((bf16[32,4096]{1,0:T(8,128)(2,1)S(1)}, bf16[32,4096]{1,0:T(8,128)(2,1)S(1)}, u32[]{:S(2)}, u32[]{:S(2)}) %collective-permute-start.3) | collective-permute-done | bytes 262176 | tf_op jit(solution)/shard_map/ppermute | solution.py:167
  20.4 0.0 copy-start.3
  20.4 0.8 copy-done.3
  21.3 1.0 arrange.1.tokens
  22.2 0.0 copy-start
  22.2 1.0 copy-done
  23.3 1.0 copy-done.1
  24.3 7.6 %share.7 = f32[2,64,1024]{2,1,0:T(8,128)S(1)} custom-call(s32[4]{0:T(128)S(1)} %get-tuple-element.22.where, bf16[3,64,2048]{2,1,0:T(8,128)(2,1)S(1)} %arrange.1.tokens, bf16[2048,4096]{1,0:T(8,128)(2,1)} %gate.7, bf16[2048,4096]{1,0:T(8,128)(2,1)} %up.7, s32[32,4096]{1,0:T(8,128)S(1)} %copy-done, s32[32,4096]{1,0:T(8,128)S(1)} %copy-done.1), custom_call_target="tpu_custom_call" | custom-call | flops 1610612736 | bytes 8388608 | tf_op jit(solution)/shard_map/share/pallas_call | solution.py:23
  31.9 0.1 collective-permute-start.5
  32.0 7.6 %share.5 = f32[2,64,1024]{2,1,0:T(8,128)S(1)} custom-call(s32[4]{0:T(128)S(1)} %get-tuple-element.14.where, bf16[3,64,2048]{2,1,0:T(8,128)(2,1)S(1)} %arrange.1.tokens, bf16[2048,4096]{1,0:T(8,128)(2,1)} %gate.7, bf16[2048,4096]{1,0:T(8,128)(2,1)} %up.7, s32[32,4096]{1,0:T(8,128)S(1)} %copy-done, s32[32,4096]{1,0:T(8,128)S(1)} %copy-done.1), custom_call_target="tpu_custom_call" | custom-call | flops 1610612736 | bytes 8388608 | tf_op jit(solution)/shard_map/share/pallas_call | solution.py:23
  39.6 0.6 collective-permute-start.4
  40.2 7.6 %share.6 = f32[2,64,1024]{2,1,0:T(8,128)S(1)} custom-call(s32[4]{0:T(128)S(1)} %get-tuple-element.21.where, bf16[3,64,2048]{2,1,0:T(8,128)(2,1)S(1)} %arrange.1.tokens, bf16[2048,4096]{1,0:T(8,128)(2,1)} %gate.7, bf16[2048,4096]{1,0:T(8,128)(2,1)} %up.7, s32[32,4096]{1,0:T(8,128)S(1)} %copy-done, s32[32,4096]{1,0:T(8,128)S(1)} %copy-done.2), custom_call_target="tpu_custom_call" | custom-call | flops 1610612736 | bytes 8388608 | tf_op jit(solution)/shard_map/share/pallas_call | solution.py:23
  47.8 0.1 add.88
  47.9 1.7 %collective-permute-start.6 = (f32[2,64,1024]{2,1,0:T(8,128)S(1)}, f32[2,64,1024]{2,1,0:T(8,128)S(1)}, u32[]{:S(2)}, u32[]{:S(2)}) collective-permute-start(f32[2,64,1024]{2,1,0:T(8,128)S(1)} %add.88), channel_id=1, source_target_pairs={{0,2},{1,3},{2,0},{3,1},{4,6},{5,7},{6,4},{7,5},{8,10},{9,11},{10,... | collective-permute-start | bytes 1572872 | tf_op jit(solution)/shard_map/ppermute | solution.py:169
  49.6 7.6 %share.4 = f32[2,64,1024]{2,1,0:T(8,128)S(1)} custom-call(s32[4]{0:T(128)S(1)} %get-tuple-element.20.where, bf16[3,64,2048]{2,1,0:T(8,128)(2,1)S(1)} %arrange.1.tokens, bf16[2048,4096]{1,0:T(8,128)(2,1)} %gate.7, bf16[2048,4096]{1,0:T(8,128)(2,1)} %up.7, s32[32,4096]{1,0:T(8,128)S(1)} %copy-done, s32[32,4096]{1,0:T(8,128)S(1)} %copy-done.2), custom_call_target="tpu_custom_call" | custom-call | flops 1610612736 | bytes 8388608 | tf_op jit(solution)/shard_map/share/pallas_call | solution.py:23
  57.2 0.0 collective-permute-done.4
  57.2 4.6 %collective-permute-done.6 = f32[2,64,1024]{2,1,0:T(8,128)S(1)} collective-permute-done((f32[2,64,1024]{2,1,0:T(8,128)S(1)}, f32[2,64,1024]{2,1,0:T(8,128)S(1)}, u32[]{:S(2)}, u32[]{:S(2)}) %collective-permute-start.6) | collective-permute-done | bytes 524320 | tf_op jit(solution)/shard_map/ppermute | solution.py:169
  61.8 0.1 add_add_fusion
  61.9 0.1 fusion.1.refs_0_
  62.0 1.7 %collective-permute-start.7 = (bf16[64,1024]{1,0:T(8,128)(2,1)S(1)}, bf16[64,1024]{1,0:T(8,128)(2,1)S(1)}, u32[]{:S(2)}, u32[]{:S(2)}) collective-permute-start(bf16[64,1024]{1,0:T(8,128)(2,1)S(1)} %fusion.1.refs_0_), channel_id=1, source_target_pairs={{0,2},{1,3},{2,0},{3,1},{4,6},{5,7},{6,4},{7,5},{8,10},{9,11},{10,... | collective-permute-start | bytes 393224 | tf_op jit(solution)/shard_map/ppermute | solution.py:169
  63.7 0.0 collective-permute-start.9
  63.7 3.4 %collective-permute-done.7.refs_0_ = bf16[64,1024]{1,0:T(8,128)(2,1)S(1)} collective-permute-done((bf16[64,1024]{1,0:T(8,128)(2,1)S(1)}, bf16[64,1024]{1,0:T(8,128)(2,1)S(1)}, u32[]{:S(2)}, u32[]{:S(2)}) %collective-permute-start.7) | collective-permute-done | bytes 131104 | tf_op jit(solution)/shard_map/ppermute | solution.py:169
  67.0 0.0 collective-permute-start.8
  67.0 0.1 stack.102.where
  67.1 0.1 stack.104.where
  67.2 0.0 collective-permute-done.9.refs_1_
  67.2 9.9 %down.3.refs_4_ = f32[64,4096]{1,0:T(8,128)S(1)} custom-call(s32[6]{0:T(128)S(1)} %stack.102.where, bf16[64,1024]{1,0:T(8,128)(2,1)S(1)} %fusion.1.refs_0_, bf16[64,1024]{1,0:T(8,128)(2,1)S(1)} %collective-permute-done.9.refs_1_, bf16[4096,4096]{1,0:T(8,128)(2,1)} %refs_3_.5, bf16[4096,4096]{1,0:T(8,128)(2,1)} %refs_3_.5), custom_call_target="tpu_custom_call" | custom-call | flops 1073741824 | bytes 16777216 | tf_op jit(solution)/shard_map/down/pallas_call | solution.py:23
  77.1 0.0 collective-permute-done.8.refs_1_
  77.1 5.5 %down.5 = bf16[64,2048]{1,0:T(8,128)(2,1)S(1)} custom-call(s32[6]{0:T(128)S(1)} %stack.104.where, bf16[64,1024]{1,0:T(8,128)(2,1)S(1)} %collective-permute-done.7.refs_0_, bf16[64,1024]{1,0:T(8,128)(2,1)S(1)} %collective-permute-done.8.refs_1_, bf16[4096,4096]{1,0:T(8,128)(2,1)} %refs_3_.5, bf16[4096,4096]{1,0:T(8,128)(2,1)} %refs_3_.5, ...), custom_call_target="tpu_custom_call" | custom-call | flops 536870912 | bytes 8388608 | tf_op jit(solution)/shard_map/down/pallas_call | solution.py:23
  82.7 1.7 %collective-permute-start.10 = (bf16[64,2048]{1,0:T(8,128)(2,1)S(1)}, bf16[64,2048]{1,0:T(8,128)(2,1)S(1)}, u32[]{:S(2)}, u32[]{:S(2)}) collective-permute-start(bf16[64,2048]{1,0:T(8,128)(2,1)S(1)} %down.5), channel_id=1, source_target_pairs={{0,4},{4,0},{8,12},{12,8},{16,20},{20,16},{24,28},{28,24},{1,5},{5... | collective-permute-start | bytes 786440 | tf_op jit(solution)/shard_map/ppermute | solution.py:167
  84.4 0.1 stack.91.where
  84.4 5.5 %down.4.mine = f32[64,2048]{1,0:T(8,128)S(1)} custom-call(s32[6]{0:T(128)S(1)} %stack.91.where, bf16[64,1024]{1,0:T(8,128)(2,1)S(1)} %collective-permute-done.7.refs_0_, bf16[64,1024]{1,0:T(8,128)(2,1)S(1)} %collective-permute-done.8.refs_1_, bf16[4096,4096]{1,0:T(8,128)(2,1)} %refs_3_.5, bf16[4096,4096]{1,0:T(8,128)(2,1)} %refs_3_.5, ...), custom_call_target="tpu_custom_call" | custom-call | flops 536870912 | bytes 8388608 | tf_op jit(solution)/shard_map/down/pallas_call | solution.py:23
  90.0 1.4 %collective-permute-done.10.theirs = bf16[64,2048]{1,0:T(8,128)(2,1)S(1)} collective-permute-done((bf16[64,2048]{1,0:T(8,128)(2,1)S(1)}, bf16[64,2048]{1,0:T(8,128)(2,1)S(1)}, u32[]{:S(2)}, u32[]{:S(2)}) %collective-permute-start.10) | collective-permute-done | bytes 262176 | tf_op jit(solution)/shard_map/ppermute | solution.py:167
  91.4 0.6 split.1
  92.1 0.2 collective-permute-start.11
  92.3 2.0 %collective-permute-start.12 = (bf16[16,2048]{1,0:T(8,128)(2,1)S(1)}, bf16[16,2048]{1,0:T(8,128)(2,1)S(1)}, u32[]{:S(2)}, u32[]{:S(2)}) collective-permute-start(bf16[16,2048]{1,0:T(8,128)(2,1)S(1)} %get-tuple-element.10), channel_id=1, source_target_pairs={{0,16},{4,20},{8,24},{12,28},{16,0},{20,4},{24,8},{28,12},{1,17},{... | collective-permute-start | bytes 196616 | tf_op jit(solution)/shard_map/ppermute | solution.py:170
  94.3 2.2 %collective-permute-start.13 = (bf16[16,2048]{1,0:T(8,128)(2,1)S(1)}, bf16[16,2048]{1,0:T(8,128)(2,1)S(1)}, u32[]{:S(2)}, u32[]{:S(2)}) collective-permute-start(bf16[16,2048]{1,0:T(8,128)(2,1)S(1)} %get-tuple-element.11), channel_id=1, source_target_pairs={{0,24},{4,28},{8,16},{12,20},{16,8},{20,12},{24,0},{28,4},{1,25},{... | collective-permute-start | bytes 196616 | tf_op jit(solution)/shard_map/ppermute | solution.py:170
  96.5 0.2 collective-permute-done.11.refs_1_
  96.7 2.8 %collective-permute-done.12.refs_2_ = bf16[16,2048]{1,0:T(8,128)(2,1)S(1)} collective-permute-done((bf16[16,2048]{1,0:T(8,128)(2,1)S(1)}, bf16[16,2048]{1,0:T(8,128)(2,1)S(1)}, u32[]{:S(2)}, u32[]{:S(2)}) %collective-permute-start.12) | collective-permute-done | bytes 65568 | tf_op jit(solution)/shard_map/ppermute | solution.py:170
  99.6 0.8 collective-permute-done.13.refs_3_
  100.4 0.6 finish.1.refs_0_
  100.9 2.4 %collective-permute-start.16 = (bf16[16,2048]{1,0:T(8,128)(2,1)S(1)}, bf16[16,2048]{1,0:T(8,128)(2,1)S(1)}, u32[]{:S(2)}, u32[]{:S(2)}) collective-permute-start(bf16[16,2048]{1,0:T(8,128)(2,1)S(1)} %finish.1.refs_0_), channel_id=1, source_target_pairs={{0,24},{4,28},{8,16},{12,20},{16,8},{20,12},{24,0},{28,4},{1,25},{... | collective-permute-start | bytes 196616 | tf_op jit(solution)/shard_map/ppermute | solution.py:170
  103.3 0.3 collective-permute-start.15
  103.6 1.8 %collective-permute-start.14 = (bf16[16,2048]{1,0:T(8,128)(2,1)S(1)}, bf16[16,2048]{1,0:T(8,128)(2,1)S(1)}, u32[]{:S(2)}, u32[]{:S(2)}) collective-permute-start(bf16[16,2048]{1,0:T(8,128)(2,1)S(1)} %finish.1.refs_0_), channel_id=1, source_target_pairs={{0,8},{4,12},{8,0},{12,4},{16,24},{20,28},{24,16},{28,20},{1,9},{5... | collective-permute-start | bytes 196616 | tf_op jit(solution)/shard_map/ppermute | solution.py:170
  105.4 2.0 %collective-permute-done.16.refs_3_ = bf16[16,2048]{1,0:T(8,128)(2,1)S(1)} collective-permute-done((bf16[16,2048]{1,0:T(8,128)(2,1)S(1)}, bf16[16,2048]{1,0:T(8,128)(2,1)S(1)}, u32[]{:S(2)}, u32[]{:S(2)}) %collective-permute-start.16) | collective-permute-done | bytes 65568 | tf_op jit(solution)/shard_map/ppermute | solution.py:170
  107.4 1.4 %collective-permute-done.15.refs_2_ = bf16[16,2048]{1,0:T(8,128)(2,1)S(1)} collective-permute-done((bf16[16,2048]{1,0:T(8,128)(2,1)S(1)}, bf16[16,2048]{1,0:T(8,128)(2,1)S(1)}, u32[]{:S(2)}, u32[]{:S(2)}) %collective-permute-start.15) | collective-permute-done | bytes 65568 | tf_op jit(solution)/shard_map/ppermute | solution.py:170
  108.8 0.6 join.1.own
  109.4 3.4 %collective-permute-start.18 = (bf16[64,2048]{1,0:T(8,128)(2,1)S(1)}, bf16[64,2048]{1,0:T(8,128)(2,1)S(1)}, u32[]{:S(2)}, u32[]{:S(2)}) collective-permute-start(bf16[64,2048]{1,0:T(8,128)(2,1)S(1)} %broadcast_select_fusion), channel_id=1, source_target_pairs={{0,2},{4,6},{9,11},{13,15},{18,16},{22,20},{27,25},{31,29}} | collective-permute-start | bytes 786440 | tf_op jit(solution)/shard_map/ppermute | solution.py:278
  112.9 3.9 %collective-permute-done.18 = bf16[64,2048]{1,0:T(8,128)(2,1)S(1)} collective-permute-done((bf16[64,2048]{1,0:T(8,128)(2,1)S(1)}, bf16[64,2048]{1,0:T(8,128)(2,1)S(1)}, u32[]{:S(2)}, u32[]{:S(2)}) %collective-permute-start.18) | collective-permute-done | bytes 262176 | tf_op jit(solution)/shard_map/ppermute | solution.py:278
  116.7 0.1 collective-permute-start.19
  116.8 1.6 %collective-permute-start.17 = (bf16[64,2048]{1,0:T(8,128)(2,1)S(1)}, bf16[64,2048]{1,0:T(8,128)(2,1)S(1)}, u32[]{:S(2)}, u32[]{:S(2)}) collective-permute-start(bf16[64,2048]{1,0:T(8,128)(2,1)S(1)} %join.1.own), channel_id=1, source_target_pairs={{0,4},{4,0},{8,12},{12,8},{16,20},{20,16},{24,28},{28,24},{1,5},{5... | collective-permute-start | bytes 786440 | tf_op jit(solution)/shard_map/ppermute | solution.py:167
  118.4 0.0 collective-permute-done.19
  118.5 7.1 %collective-permute-done.17.other = bf16[64,2048]{1,0:T(8,128)(2,1)S(1)} collective-permute-done((bf16[64,2048]{1,0:T(8,128)(2,1)S(1)}, bf16[64,2048]{1,0:T(8,128)(2,1)S(1)}, u32[]{:S(2)}, u32[]{:S(2)}) %collective-permute-start.17) | collective-permute-done | bytes 262176 | tf_op jit(solution)/shard_map/ppermute | solution.py:167
  125.5 13.0 %gram.1 = (f32[4096,2048]{1,0:T(8,128)}, bf16[8,4096]{1,0:T(8,128)(2,1)}) custom-call(s32[3]{0:T(128)S(1)} %pad_add_fusion.where, bf16[64,2048]{1,0:T(8,128)(2,1)S(1)} %join.1.own, bf16[64,2048]{1,0:T(8,128)(2,1)S(1)} %collective-permute-done.17.other, bf16[64,2048]{1,0:T(8,128)(2,1)S(1)} %select_add_fusion.columns), custom_call_target="tpu_custom_call" | custom-call | flops 1073741824 | bytes 33554432 | tf_op jit(solution)/shard_map/gram/pallas_call | solution.py:23
  (10 shorter events, 0.1 us)
Async XLA Ops:
  0.6 7.9 %collective-permute-start.2 = (bf16[8,4096]{1,0:T(8,128)(2,1)}, bf16[8,4096]{1,0:T(8,128)(2,1)S(1)}, u32[]{:S(2)}, u32[]{:S(2)}) collective-permute-start(bf16[8,4096]{1,0:T(8,128)(2,1)} %refs_0_.1), channel_id=1, source_target_pairs={{0,24},{4,28},{8,16},{12,20},{16,8},{20,12},{24,0},{28,4},{1,25},{... | collective-permute-start | bytes 196616 | tf_op jit(solution)/shard_map/ppermute | solution.py:170
  5.8 5.8 %collective-permute-start.1 = (bf16[8,4096]{1,0:T(8,128)(2,1)}, bf16[8,4096]{1,0:T(8,128)(2,1)S(1)}, u32[]{:S(2)}, u32[]{:S(2)}) collective-permute-start(bf16[8,4096]{1,0:T(8,128)(2,1)} %refs_0_.1), channel_id=1, source_target_pairs={{0,16},{4,20},{8,24},{12,28},{16,0},{20,4},{24,8},{28,12},{1,17},{... | collective-permute-start | bytes 196616 | tf_op jit(solution)/shard_map/ppermute | solution.py:170
  5.8 5.8 %collective-permute-start = (bf16[8,4096]{1,0:T(8,128)(2,1)}, bf16[8,4096]{1,0:T(8,128)(2,1)S(1)}, u32[]{:S(2)}, u32[]{:S(2)}) collective-permute-start(bf16[8,4096]{1,0:T(8,128)(2,1)} %refs_0_.1), channel_id=1, source_target_pairs={{0,8},{4,12},{8,0},{12,4},{16,24},{20,28},{24,16},{28,20},{1,9},{5... | collective-permute-start | bytes 196616 | tf_op jit(solution)/shard_map/ppermute | solution.py:170
  12.5 7.9 %collective-permute-start.3 = (bf16[32,4096]{1,0:T(8,128)(2,1)S(1)}, bf16[32,4096]{1,0:T(8,128)(2,1)S(1)}, u32[]{:S(2)}, u32[]{:S(2)}) collective-permute-start(bf16[32,4096]{1,0:T(8,128)(2,1)S(1)} %pad_maximum_fusion), channel_id=1, source_target_pairs={{0,4},{4,0},{8,12},{12,8},{16,20},{20,16},{24,28},{28,24},{1,5},{5... | collective-permute-start | bytes 786440 | tf_op jit(solution)/shard_map/ppermute | solution.py:167
  20.4 0.8 copy-start.3
  22.2 1.0 copy-start
  23.3 1.0 copy-start.1
  24.3 15.9 %copy-start.2 = (s32[32,4096]{1,0:T(8,128)S(1)}, s32[32,4096]{1,0:T(8,128)}, u32[]{:S(2)}) copy-start(s32[32,4096]{1,0:T(8,128)} %up_code.7) | copy-start | bytes 1572868
  31.9 15.9 %collective-permute-start.5 = (f32[2,64,1024]{2,1,0:T(8,128)S(1)}, f32[2,64,1024]{2,1,0:T(8,128)S(1)}, u32[]{:S(2)}, u32[]{:S(2)}) collective-permute-start(f32[2,64,1024]{2,1,0:T(8,128)S(1)} %share.7), channel_id=1, source_target_pairs={{0,1},{1,0},{2,3},{3,2},{4,5},{5,4},{6,7},{7,6},{8,9},{9,8},{10,11... | collective-permute-start | bytes 1572872 | tf_op jit(solution)/shard_map/ppermute | solution.py:168
  39.6 17.5 %collective-permute-start.4 = (f32[2,64,1024]{2,1,0:T(8,128)S(1)}, f32[2,64,1024]{2,1,0:T(8,128)S(1)}, u32[]{:S(2)}, u32[]{:S(2)}) collective-permute-start(f32[2,64,1024]{2,1,0:T(8,128)S(1)} %share.5), channel_id=1, source_target_pairs={{0,1},{1,0},{2,3},{3,2},{4,5},{5,4},{6,7},{7,6},{8,9},{9,8},{10,11... | collective-permute-start | bytes 1572872 | tf_op jit(solution)/shard_map/ppermute | solution.py:168
  47.9 13.9 %collective-permute-start.6 = (f32[2,64,1024]{2,1,0:T(8,128)S(1)}, f32[2,64,1024]{2,1,0:T(8,128)S(1)}, u32[]{:S(2)}, u32[]{:S(2)}) collective-permute-start(f32[2,64,1024]{2,1,0:T(8,128)S(1)} %add.88), channel_id=1, source_target_pairs={{0,2},{1,3},{2,0},{3,1},{4,6},{5,7},{6,4},{7,5},{8,10},{9,11},{10,... | collective-permute-start | bytes 1572872 | tf_op jit(solution)/shard_map/ppermute | solution.py:169
  62.0 5.0 %collective-permute-start.7 = (bf16[64,1024]{1,0:T(8,128)(2,1)S(1)}, bf16[64,1024]{1,0:T(8,128)(2,1)S(1)}, u32[]{:S(2)}, u32[]{:S(2)}) collective-permute-start(bf16[64,1024]{1,0:T(8,128)(2,1)S(1)} %fusion.1.refs_0_), channel_id=1, source_target_pairs={{0,2},{1,3},{2,0},{3,1},{4,6},{5,7},{6,4},{7,5},{8,10},{9,11},{10,... | collective-permute-start | bytes 393224 | tf_op jit(solution)/shard_map/ppermute | solution.py:169
  63.7 3.5 %collective-permute-start.9 = (bf16[64,1024]{1,0:T(8,128)(2,1)S(1)}, bf16[64,1024]{1,0:T(8,128)(2,1)S(1)}, u32[]{:S(2)}, u32[]{:S(2)}) collective-permute-start(bf16[64,1024]{1,0:T(8,128)(2,1)S(1)} %fusion.1.refs_0_), channel_id=1, source_target_pairs={{0,1},{1,0},{2,3},{3,2},{4,5},{5,4},{6,7},{7,6},{8,9},{9,8},{10,11... | collective-permute-start | bytes 393224 | tf_op jit(solution)/shard_map/ppermute | solution.py:168
  67.0 10.1 %collective-permute-start.8 = (bf16[64,1024]{1,0:T(8,128)(2,1)S(1)}, bf16[64,1024]{1,0:T(8,128)(2,1)S(1)}, u32[]{:S(2)}, u32[]{:S(2)}) collective-permute-start(bf16[64,1024]{1,0:T(8,128)(2,1)S(1)} %collective-permute-done.7.refs_0_), channel_id=1, source_target_pairs={{0,1},{1,0},{2,3},{3,2},{4,5},{5,4},{6,7},{7,6},{8,9},{9,8},{10,11... | collective-permute-start | bytes 393224 | tf_op jit(solution)/shard_map/ppermute | solution.py:168
  82.7 8.8 %collective-permute-start.10 = (bf16[64,2048]{1,0:T(8,128)(2,1)S(1)}, bf16[64,2048]{1,0:T(8,128)(2,1)S(1)}, u32[]{:S(2)}, u32[]{:S(2)}) collective-permute-start(bf16[64,2048]{1,0:T(8,128)(2,1)S(1)} %down.5), channel_id=1, source_target_pairs={{0,4},{4,0},{8,12},{12,8},{16,20},{20,16},{24,28},{28,24},{1,5},{5... | collective-permute-start | bytes 786440 | tf_op jit(solution)/shard_map/ppermute | solution.py:167
  92.1 4.7 %collective-permute-start.11 = (bf16[16,2048]{1,0:T(8,128)(2,1)S(1)}, bf16[16,2048]{1,0:T(8,128)(2,1)S(1)}, u32[]{:S(2)}, u32[]{:S(2)}) collective-permute-start(bf16[16,2048]{1,0:T(8,128)(2,1)S(1)} %get-tuple-element.9), channel_id=1, source_target_pairs={{0,8},{4,12},{8,0},{12,4},{16,24},{20,28},{24,16},{28,20},{1,9},{5... | collective-permute-start | bytes 196616 | tf_op jit(solution)/shard_map/ppermute | solution.py:170
  92.3 7.3 %collective-permute-start.12 = (bf16[16,2048]{1,0:T(8,128)(2,1)S(1)}, bf16[16,2048]{1,0:T(8,128)(2,1)S(1)}, u32[]{:S(2)}, u32[]{:S(2)}) collective-permute-start(bf16[16,2048]{1,0:T(8,128)(2,1)S(1)} %get-tuple-element.10), channel_id=1, source_target_pairs={{0,16},{4,20},{8,24},{12,28},{16,0},{20,4},{24,8},{28,12},{1,17},{... | collective-permute-start | bytes 196616 | tf_op jit(solution)/shard_map/ppermute | solution.py:170
  94.3 6.1 %collective-permute-start.13 = (bf16[16,2048]{1,0:T(8,128)(2,1)S(1)}, bf16[16,2048]{1,0:T(8,128)(2,1)S(1)}, u32[]{:S(2)}, u32[]{:S(2)}) collective-permute-start(bf16[16,2048]{1,0:T(8,128)(2,1)S(1)} %get-tuple-element.11), channel_id=1, source_target_pairs={{0,24},{4,28},{8,16},{12,20},{16,8},{20,12},{24,0},{28,4},{1,25},{... | collective-permute-start | bytes 196616 | tf_op jit(solution)/shard_map/ppermute | solution.py:170
  100.9 6.5 %collective-permute-start.16 = (bf16[16,2048]{1,0:T(8,128)(2,1)S(1)}, bf16[16,2048]{1,0:T(8,128)(2,1)S(1)}, u32[]{:S(2)}, u32[]{:S(2)}) collective-permute-start(bf16[16,2048]{1,0:T(8,128)(2,1)S(1)} %finish.1.refs_0_), channel_id=1, source_target_pairs={{0,24},{4,28},{8,16},{12,20},{16,8},{20,12},{24,0},{28,4},{1,25},{... | collective-permute-start | bytes 196616 | tf_op jit(solution)/shard_map/ppermute | solution.py:170
  103.3 5.5 %collective-permute-start.15 = (bf16[16,2048]{1,0:T(8,128)(2,1)S(1)}, bf16[16,2048]{1,0:T(8,128)(2,1)S(1)}, u32[]{:S(2)}, u32[]{:S(2)}) collective-permute-start(bf16[16,2048]{1,0:T(8,128)(2,1)S(1)} %finish.1.refs_0_), channel_id=1, source_target_pairs={{0,16},{4,20},{8,24},{12,28},{16,0},{20,4},{24,8},{28,12},{1,17},{... | collective-permute-start | bytes 196616 | tf_op jit(solution)/shard_map/ppermute | solution.py:170
  103.6 5.2 %collective-permute-start.14 = (bf16[16,2048]{1,0:T(8,128)(2,1)S(1)}, bf16[16,2048]{1,0:T(8,128)(2,1)S(1)}, u32[]{:S(2)}, u32[]{:S(2)}) collective-permute-start(bf16[16,2048]{1,0:T(8,128)(2,1)S(1)} %finish.1.refs_0_), channel_id=1, source_target_pairs={{0,8},{4,12},{8,0},{12,4},{16,24},{20,28},{24,16},{28,20},{1,9},{5... | collective-permute-start | bytes 196616 | tf_op jit(solution)/shard_map/ppermute | solution.py:170
  109.4 7.3 %collective-permute-start.18 = (bf16[64,2048]{1,0:T(8,128)(2,1)S(1)}, bf16[64,2048]{1,0:T(8,128)(2,1)S(1)}, u32[]{:S(2)}, u32[]{:S(2)}) collective-permute-start(bf16[64,2048]{1,0:T(8,128)(2,1)S(1)} %broadcast_select_fusion), channel_id=1, source_target_pairs={{0,2},{4,6},{9,11},{13,15},{18,16},{22,20},{27,25},{31,29}} | collective-permute-start | bytes 786440 | tf_op jit(solution)/shard_map/ppermute | solution.py:278
  116.7 1.7 %collective-permute-start.19 = (bf16[64,2048]{1,0:T(8,128)(2,1)S(1)}, bf16[64,2048]{1,0:T(8,128)(2,1)S(1)}, u32[]{:S(2)}, u32[]{:S(2)}) collective-permute-start(bf16[64,2048]{1,0:T(8,128)(2,1)S(1)} %fusion.3), channel_id=1, source_target_pairs={{0,1},{1,0},{2,3},{3,2},{4,5},{5,4},{6,7},{7,6},{8,9},{9,8},{10,11... | collective-permute-start | bytes 786440 | tf_op jit(solution)/shard_map/ppermute | solution.py:168
  116.8 8.7 %collective-permute-start.17 = (bf16[64,2048]{1,0:T(8,128)(2,1)S(1)}, bf16[64,2048]{1,0:T(8,128)(2,1)S(1)}, u32[]{:S(2)}, u32[]{:S(2)}) collective-permute-start(bf16[64,2048]{1,0:T(8,128)(2,1)S(1)} %join.1.own), channel_id=1, source_target_pairs={{0,4},{4,0},{8,12},{12,8},{16,20},{20,16},{24,28},{28,24},{1,5},{5... | collective-permute-start | bytes 786440 | tf_op jit(solution)/shard_map/ppermute | solution.py:167

commit v2 on v1

v2 whole, which is shorter than its diff:
```python
import functools
import math

import jax
import jax.numpy as jnp
from jax import lax
from jax.experimental import pallas as pl
from jax.experimental.pallas import tpu as pltpu
from jax.sharding import PartitionSpec as P


F32, BF16 = jnp.float32, jnp.bfloat16
ROWS, GROUP = 128, 4
MIB = 1 << 20


def tile(limit, width):
    return limit if width % limit == 0 else width


def call(kernel, grid, scalars, inputs, outputs, scratch=(), cost=(0, 0), vmem=4):
    arrays, in_specs = zip(*inputs)
    shapes, out_specs = zip(*outputs)
    return pl.pallas_call(
        kernel,
        grid_spec=pltpu.PrefetchScalarGridSpec(
            num_scalar_prefetch=1,
            grid=grid,
            in_specs=list(in_specs),
            out_specs=list(out_specs),
            scratch_shapes=list(scratch),
        ),
        out_shape=list(shapes),
        cost_estimate=pl.CostEstimate(flops=cost[0], bytes_accessed=cost[1], transcendentals=0),
        compiler_params=pltpu.CompilerParams(vmem_limit_bytes=vmem * MIB),
    )(scalars, *arrays)


def whole(shape):
    return pl.BlockSpec(shape, lambda *_: (0,) * len(shape))


def arrange_kernel(deep_axis, near, where, *refs):
    own, other, out = refs[:deep_axis], refs[deep_axis:2 * deep_axis], refs[2 * deep_axis]
    deep = 2 * ROWS
    row = lax.broadcasted_iota(jnp.int32, (deep, 3 * ROWS), 0)
    column = lax.broadcasted_iota(jnp.int32, (deep, 3 * ROWS), 1)
    kind, lane = column // ROWS, column % ROWS
    block, group, second = lane // (ROWS // 2), (lane % (ROWS // 2)) // 2, lane % 2
    place = jnp.where(second == 0, kind, 3 - kind)
    mix = jnp.where(row == block * ROWS + group * GROUP + place, 1.0, 0.0).astype(BF16)
    chunks = own[0].shape[1] // deep
    first = (where[2] == 0) if near else True
    for k in range(deep_axis):
        a, b = own[k][...].astype(F32), other[k][...].astype(F32)
        both = jnp.concatenate((jnp.where(first, a, b), jnp.where(first, b, a)), axis=0).astype(BF16)
        rows = both.shape[0]
        flat = jnp.concatenate([both[:, deep * i:deep * (i + 1)] for i in range(chunks)], axis=0)
        mixed = jnp.dot(flat, mix, preferred_element_type=F32).astype(BF16)
        at = pl.multiple_of(((where[1] ^ k) if near else k) * rows, rows)
        for i in range(chunks):
            for n in range(3):
                out[n, pl.ds(at, rows), ROWS * i:ROWS * (i + 1)] = mixed[rows * i:rows * (i + 1), ROWS * n:ROWS * (n + 1)]


def share_kernel(across, ahead, turn, where, tokens, gate, up, gate_code, up_code, out, held, held_code, place, here, code_here):
    depth, share = held.shape[1:]
    blocks = held_code.shape[1]
    kept = depth // blocks
    many = 4 if blocks % 4 == 0 else 1
    span = many * kept
    lanes = tile(512, share)
    start = pl.multiple_of((lax.rem(where[3] + ahead, across) * 2 + (where[4] ^ turn)) * share, share)
    piece, ahead_by = tile(512, depth), 4
    code_copies = [
        pltpu.make_async_copy(source.at[:, pl.ds(start, share)], held_code.at[side], code_here.at[side])
        for side, source in enumerate((gate_code, up_code))
    ]
    copies, index = [], {}
    for side, source in enumerate((gate, up)):
        for at in range(0, share, lanes):
            for row in range(0, depth, piece):
                index[side, at, row] = len(copies)
                copies.append(pltpu.make_async_copy(
                    source.at[pl.ds(row, piece), pl.ds(start + at, lanes)],
                    held.at[side, pl.ds(row, piece), pl.ds(at, lanes)], here.at[len(copies)],
                ))
    code_copies[0].start()
    for copy in copies[:ahead_by]:
        copy.start()
    code_copies[1].start()
    even = lax.broadcasted_iota(jnp.int32, (16, lanes), 0) % 2 == 0
    for side in range(2):
        code_copies[side].wait()
        code = held_code[side]
        place[side, 0] = jnp.where(code < 3, 0.0, jnp.where(code < 5, 1.0, 2.0))
        place[side, 1] = jnp.where(code == 0, 2.0, jnp.where((code == 1) | (code == 3), 1.0, 0.0))
        for at in range(0, share, lanes):
            part_lanes = slice(at, at + lanes)
            total = jnp.zeros((out.shape[1], lanes), F32)
            for row in range(0, depth, span):
                number = index.get((side, at, row))
                if number is not None:
                    copies[number].wait()
                    if number + ahead_by < len(copies):
                        copies[number + ahead_by].start()
                parts = ([], [], [])
                for k in range(row // kept, (row + span) // kept):
                    first = jnp.broadcast_to(place[side, 0, pl.ds(k, 1), part_lanes], (16, lanes))
                    second = jnp.broadcast_to(place[side, 1, pl.ds(k, 1), part_lanes], (16, lanes))
                    kind = jnp.where(even, first, second)
                    value = held[side, kept * k:kept * (k + 1), part_lanes]
                    for n in range(3):
                        mask = jnp.where(kind == n, 1.0, 0.0).astype(BF16)
                        parts[n].append(value * jnp.concatenate([mask] * (kept // 16), axis=0))
                for n in range(3):
                    part = jnp.concatenate(parts[n], axis=0)
                    total = total + jnp.dot(tokens[n, :, row:row + span], part, preferred_element_type=F32)
            out[side, :, part_lanes] = total


def fetch_kernel(across, ahead, where, source, out, arrived):
    pieces = arrived.shape[0]
    rows = out.shape[0] // pieces
    start = lax.rem(where[3] + (across - ahead), across) * out.shape[0]
    copies = [
        pltpu.make_async_copy(
            source.at[pl.ds(pl.multiple_of(start + rows * i, rows), rows), :], out.at[pl.ds(rows * i, rows), :], arrived.at[i]
        )
        for i in range(pieces)
    ]
    for copy in copies:
        copy.start()
    for copy in copies:
        copy.wait()


def down_kernel(runs, side, where, own, beside, weights, *rest):
    adds, out = rest[:-1], rest[-1]
    share = own.shape[1]
    full = weights.shape[1]
    run = full // (2 * runs)
    lanes = tile(512, run)
    for i in range(out.shape[1] // lanes):
        at = i * lanes
        if side is not None:
            column = pl.ds(pl.multiple_of((2 * (at // run) + (where[2] ^ side)) * run + at % run, lanes), lanes)
        else:
            column = pl.ds(at, lanes)
        total = adds[0][:, column] if adds else None
        for left, core in ((own, where[4]), (beside, where[4] ^ 1)):
            right = weights[pl.ds(pl.multiple_of(core * share, share), share), column]
            product = jnp.dot(left[...], right, preferred_element_type=F32)
            total = product if total is None else total + product
        out[:, pl.ds(at, lanes)] = total.astype(out.dtype)


def split_kernel(where, mine, theirs, *outs):
    rows = outs[0].shape[0]
    for k, out in enumerate(outs):
        at = pl.ds(pl.multiple_of((where[1] ^ k) * rows, rows), rows)
        out[...] = (mine[at, :] + theirs[at, :].astype(F32)).astype(out.dtype)


def finish_kernel(where, *refs):
    total = refs[0][...]
    for ref in refs[1:-1]:
        total = total + ref[...].astype(F32)
    refs[-1][...] = total.astype(BF16)


def join_kernel(where, *refs):
    out = refs[-1]
    rows = refs[0].shape[0]
    for k, ref in enumerate(refs[:-1]):
        out[pl.ds(pl.multiple_of((where[1] ^ k) * rows, rows), rows), :] = ref[...]


def gram_kernel(scale, per, where, own, other, columns, out, tokens_out):
    step = pl.program_id(0)
    rows = out.shape[0]
    half = own.shape[1] // rows
    at = pl.ds(pl.multiple_of((step % half) * rows, rows), rows)
    block = jnp.where(step < half, own[:, at], other[:, at])
    product = lax.dot_general(block, columns[...], (((0,), (0,)), ((), ())), preferred_element_type=F32)
    out[...] = product * scale

    @pl.when(step == 0)
    def _():
        count = tokens_out.shape[0]
        pick = pl.ds(pl.multiple_of(where[1] * 2 * count, 2 * count), 2 * count)
        width = columns.shape[1]
        for index, ref in enumerate((own, other)):
            both = ref[pick, :].astype(F32)
            lines = jnp.where(where[2] == 0, both[:count], both[count:]).astype(BF16)
            for j in range(per):
                side = where[2] ^ index
                to = pl.ds(pl.multiple_of((2 * j + side) * width, width), width)
                tokens_out[:, to] = lines[:, width * j:width * (j + 1)]


def on_device(tokens, gate_kept, up_kept, gate_keep, up_keep, down_weight):
    wide, groups = lax.axis_size("wide"), lax.axis_size("section")
    deep, across = wide // 2, groups // 2
    w, s = lax.axis_index("wide"), lax.axis_index("section")
    z, y, x, c = w // 2, w % 2, s // 2, s % 2
    near = deep <= 4
    kept_rows, local_hidden = gate_kept.shape
    blocks = gate_keep.shape[0]
    own_tokens, section_width = tokens.shape
    count = own_tokens * wide
    half = section_width // 2
    column_width = section_width * groups // wide
    runs = half // column_width

    base = jnp.stack([jnp.asarray(v, jnp.int32) for v in (w, z, y, x, c)])
    gate_kept, up_kept, gate_keep, up_keep, down_weight = (
        pltpu.with_memory_space_constraint(v, pltpu.HBM) for v in (gate_kept, up_kept, gate_keep, up_keep, down_weight)
    )
    pairs = [(i, i ^ 1) for i in range(wide)]

    swap_y = lambda v: lax.ppermute(v, "wide", pairs)
    swap_core = lambda v: lax.ppermute(v, "section", [(i, i ^ 1) for i in range(groups)])
    turn_x = lambda v, j: lax.ppermute(v, "section", [(i, (i + 2 * j) % groups) for i in range(groups)])
    hop_z = lambda v, k: lax.ppermute(v, "wide", [(i, i ^ (2 * k)) for i in range(wide)])
    lines = [[2 * i + e for i in range(deep)] for e in range(2)]

    if near:
        own = [tokens] + [hop_z(tokens, k) for k in range(1, deep)]
        stacked = swap_y(jnp.concatenate(own, axis=0))
        other = [stacked[own_tokens * k:own_tokens * (k + 1)] for k in range(deep)]
    else:
        gathered = lax.all_gather(tokens, "wide", axis=0, tiled=True).reshape(deep, 2, own_tokens, section_width)
        own = [gathered[k, 0] for k in range(deep)]
        other = [gathered[k, 1] for k in range(deep)]
    paired = jax.ShapeDtypeStruct((3, count, section_width // 2), BF16)
    (arranged,) = call(
        functools.partial(arrange_kernel, deep, near), (1,), base,
        [(v, whole(v.shape)) for v in own + other], [(paired, whole(paired.shape))],
    )

    share = local_hidden // groups
    held_rows = []
    for j in range(across):
        (rows_held,) = call(
            functools.partial(fetch_kernel, across, j), (), base, [(down_weight, pl.BlockSpec(memory_space=pltpu.HBM))],
            [(pltpu.VMEM((2 * share, section_width), BF16), pl.BlockSpec(memory_space=pltpu.VMEM))],
            [pltpu.SemaphoreType.DMA((8,))], cost=(0, 4 * share * section_width), vmem=2,
        )
        held_rows.append(pltpu.with_memory_space_constraint(rows_held, pltpu.VMEM))

    in_hbm, in_vmem = pl.BlockSpec(memory_space=pltpu.HBM), pl.BlockSpec(memory_space=pltpu.VMEM)

    def partial_share(ahead, turn):
        (out,) = call(
            functools.partial(share_kernel, across, ahead, turn), (), base,
            [(arranged, in_vmem)] + [(v, in_hbm) for v in (gate_kept, up_kept, gate_keep, up_keep)],
            [(jax.ShapeDtypeStruct((2, count, share), F32), in_vmem)],
            [pltpu.VMEM((2, kept_rows, share), BF16), pltpu.VMEM((2, blocks, share), jnp.int32),
             pltpu.VMEM((2, 2, blocks, share), F32), pltpu.SemaphoreType.DMA((2 * (share // tile(512, share)) * (kept_rows // tile(512, kept_rows)),)),
             pltpu.SemaphoreType.DMA((2,))],
            cost=(12 * count * kept_rows * share, 4 * kept_rows * share), vmem=12,
        )
        return out

    arrived = []
    for j in range(1, across + 1):
        sent = swap_core(partial_share(j, 1))
        mine = partial_share(j, 0)
        if j < across:
            arrived.append(turn_x(mine + sent, j))
    total = mine + sent
    for value in arrived:
        total = total + value
    quarter = (jax.nn.silu(total[0]) * total[1]).astype(BF16)

    def down(own, beside, weights, adds, side, dtype):
        size = section_width if side is None else half
        inputs = [(v, whole(v.shape)) for v in (own, beside)] + [(weights, pl.BlockSpec(memory_space=pltpu.VMEM))]
        if adds is not None:
            inputs.append((adds, whole(adds.shape)))
        (out,) = call(
            functools.partial(down_kernel, runs, side), (), base, inputs,
            [(jax.ShapeDtypeStruct((count, size), dtype), whole((count, size)))],
            cost=(4 * count * share * size, 4 * share * size), vmem=4,
        )
        return out

    beside = swap_core(quarter)
    far = [turn_x(quarter, j) for j in range(1, across)]
    total = down(quarter, beside, held_rows[0], None, None, F32)
    for j in range(1, across):
        value = far[j - 1]
        other_core = swap_core(value)
        if j < across - 1:
            total = down(value, other_core, held_rows[j], total, None, F32)
    sent = swap_y(down(value, other_core, held_rows[-1], total, 1, BF16))
    mine = down(value, other_core, held_rows[-1], total, 0, F32)

    rows = count // deep
    if near:
        piece = lambda dtype: (jax.ShapeDtypeStruct((rows, half), dtype), whole((rows, half)))
        parts = call(
            split_kernel, (1,), base, [(mine, whole(mine.shape)), (sent, whole(sent.shape))],
            [piece(F32)] + [piece(BF16)] * (deep - 1),
        )
        parts = [parts[0]] + [hop_z(v, k) for k, v in enumerate(parts) if k]
        (final,) = call(finish_kernel, (1,), base, [(v, whole(v.shape)) for v in parts], [piece(BF16)])
        pieces = [final] + [hop_z(final, k) for k in range(1, deep)]
        joined = jax.ShapeDtypeStruct((count, half), BF16)
        (ours,) = call(join_kernel, (1,), base, [(v, whole(v.shape)) for v in pieces], [(joined, whole(joined.shape))])
    else:
        both = (mine + sent.astype(F32)).astype(BF16)
        parts = lax.all_to_all(both, "wide", 0, 0, tiled=True, axis_index_groups=lines)
        final = jnp.sum(parts.reshape(deep, rows, half).astype(F32), axis=0).astype(BF16)
        ours = lax.all_gather(final, "wide", axis=0, tiled=True, axis_index_groups=lines)
    theirs = swap_y(ours)

    per = wide // groups
    root = [i // per for i in range(wide)]
    at_root = w // per
    held = lax.dynamic_slice_in_dim(ours, ((w % per) // 2) * column_width, column_width, 1)
    held = jnp.where(s == at_root, held, 0).astype(BF16)
    everywhere = ("wide", "section")
    same_core = held
    for j in range(1, across):
        step = [(i * groups + root[i], i * groups + (root[i] + 2 * j) % groups) for i in range(wide)]
        same_core = same_core + lax.ppermute(held, everywhere, step)
    columns = same_core + jnp.where((s ^ at_root) % 2 == 0, 0, swap_core(same_core)).astype(BF16)

    line = tile(512, column_width)
    each = column_width // line

    def natural(i, where):
        side, j = i // (half // line), i % (half // line)
        return ((j // each) * 2 + (where[2] ^ side)) * each + j % each

    gram, next_input = call(
        functools.partial(gram_kernel, 1.0 / math.sqrt(count), runs), (section_width // line,), base,
        [(ours, whole(ours.shape)), (theirs, whole(theirs.shape)), (columns, whole(columns.shape))],
        [(jax.ShapeDtypeStruct((section_width, column_width), F32), pl.BlockSpec((line, column_width), lambda i, where: (natural(i, where), 0))),
         (jax.ShapeDtypeStruct((own_tokens, section_width), BF16), whole((own_tokens, section_width)))],
        cost=(2 * count * section_width * column_width, 4 * section_width * column_width), vmem=40,
    )
    return (next_input, gram)


def solution(mesh):
    return jax.shard_map(
        on_device,
        mesh=mesh,
        in_specs=(
            P("wide", "section"),
            P("section", "wide"),
            P("section", "wide"),
            P("section", "wide"),
            P("section", "wide"),
            P("wide", "section"),
        ),
        out_specs=(P("wide", "section"), P("section", "wide")),
        check_vma=False,
    )
```

time: 139 us -> 140 us (level)
  waiting for transfers between devices: 39 us -> 44.9 us
  local copies, waits for them, and re-layouts: 3.18 us -> 0.94 us
  Pallas kernels: 67.1 us -> 65 us
    ppermute x9, waiting for transfers between devices: 12.4 us -> 15.4 us  [on_device(): lax.ppermute(v, 'wide', [(i, i ^ 2 * k) for i in range(wide)])]
    ppermute x3, waiting for transfers between devices: 14.7 us -> 16.9 us  [on_device(): swap_y = lambda v: lax.ppermute(v, 'wide', pairs)]
    pallas_call x12 -> x14, Pallas kernels: 67.1 us -> 65 us  [call(): pl.pallas_call(kernel, grid_spec=pltpu.PrefetchScalarGridSpec(num_scalar_...]
    unnamed x8 -> x2, local copies, waits for them, and re-layouts: 2.92 us -> 0.83 us
  transfers between devices with their start and end apart: 20 -> 20, of which waited for: 13 -> 13; matrix products, arithmetic and copies ran while one was open for 0% -> 0% of each run, Pallas kernels for 28% -> 29%
where the time goes in v2:
time: 140 us
  Pallas kernels  65 us (46%)
  waiting for transfers between devices  44.9 us (32%)
  starting transfers between devices  26.6 us (19%)
    pallas_call x14, Pallas kernels, call(): pl.pallas_call(kernel, grid_spec=pltpu.PrefetchScalarGridSpec(num_scalar_...  65 us
    ppermute x3, waiting for transfers between devices, on_device(): swap_y = lambda v: lax.ppermute(v, 'wide', pairs)  16.9 us
    ppermute x9, waiting for transfers between devices, on_device(): lax.ppermute(v, 'wide', [(i, i ^ 2 * k) for i in range(wide)])  15.4 us
    ppermute x9, starting transfers between devices, on_device(): lax.ppermute(v, 'wide', [(i, i ^ 2 * k) for i in range(wide)])  14.6 us
    ppermute x2, waiting for transfers between devices, on_device(): lax.ppermute(v, 'section', [(i, (i + 2 * j) % groups) for i in range(grou...  8.73 us
    ppermute x3, starting transfers between devices, on_device(): swap_y = lambda v: lax.ppermute(v, 'wide', pairs)  4.75 us
    ppermute x1, waiting for transfers between devices, on_device(): same_core = same_core + lax.ppermute(held, everywhere, step)  3.86 us
    ppermute x1, starting transfers between devices, on_device(): same_core = same_core + lax.ppermute(held, everywhere, step)  3.41 us
  transfers between devices with their start and end apart: 20, of which 13 were waited for; matrix products, arithmetic and copies ran while one was open for 0% of the time, Pallas kernels for 29%

profile of v2, /device:TPU:0, one launch (start us, length us, event | category | flops | bytes accessed | tf_op | source)
XLA Modules:
  0.0 139.5 jit_solution(6055370341499680121)
XLA Ops:
  0.6 3.1 %collective-permute-start = (bf16[8,4096]{1,0:T(8,128)(2,1)}, bf16[8,4096]{1,0:T(8,128)(2,1)S(1)}, u32[]{:S(2)}, u32[]{:S(2)}) collective-permute-start(bf16[8,4096]{1,0:T(8,128)(2,1)} %refs_0_.1), channel_id=1, source_target_pairs={{0,8},{4,12},{8,0},{12,4},{16,24},{20,28},{24,16},{28,20},{1,9},{5... | collective-permute-start | bytes 196616 | tf_op jit(solution)/shard_map/ppermute | solution.py:225
  3.7 2.6 %collective-permute-start.1 = (bf16[8,4096]{1,0:T(8,128)(2,1)}, bf16[8,4096]{1,0:T(8,128)(2,1)S(1)}, u32[]{:S(2)}, u32[]{:S(2)}) collective-permute-start(bf16[8,4096]{1,0:T(8,128)(2,1)} %refs_0_.1), channel_id=1, source_target_pairs={{0,16},{4,20},{8,24},{12,28},{16,0},{20,4},{24,8},{28,12},{1,17},{... | collective-permute-start | bytes 196616 | tf_op jit(solution)/shard_map/ppermute | solution.py:225
  6.3 0.0 collective-permute-start.2
  6.3 0.0 collective-permute-done.refs_1_
  6.3 4.9 %collective-permute-done.1.refs_2_ = bf16[8,4096]{1,0:T(8,128)(2,1)S(1)} collective-permute-done((bf16[8,4096]{1,0:T(8,128)(2,1)}, bf16[8,4096]{1,0:T(8,128)(2,1)S(1)}, u32[]{:S(2)}, u32[]{:S(2)}) %collective-permute-start.1) | collective-permute-done | bytes 65568 | tf_op jit(solution)/shard_map/ppermute | solution.py:225
  11.2 1.4 %collective-permute-done.2.refs_3_ = bf16[8,4096]{1,0:T(8,128)(2,1)S(1)} collective-permute-done((bf16[8,4096]{1,0:T(8,128)(2,1)}, bf16[8,4096]{1,0:T(8,128)(2,1)S(1)}, u32[]{:S(2)}, u32[]{:S(2)}) %collective-permute-start.2) | collective-permute-done | bytes 65568 | tf_op jit(solution)/shard_map/ppermute | solution.py:225
  12.6 0.9 pad_maximum_fusion
  13.5 1.6 %collective-permute-start.3 = (bf16[32,4096]{1,0:T(8,128)(2,1)S(1)}, bf16[32,4096]{1,0:T(8,128)(2,1)S(1)}, u32[]{:S(2)}, u32[]{:S(2)}) collective-permute-start(bf16[32,4096]{1,0:T(8,128)(2,1)S(1)} %pad_maximum_fusion), channel_id=1, source_target_pairs={{0,4},{4,0},{8,12},{12,8},{16,20},{20,16},{24,28},{28,24},{1,5},{5... | collective-permute-start | bytes 786440 | tf_op jit(solution)/shard_map/ppermute | solution.py:222
  15.1 0.1 stack.23.where
  15.2 4.8 %collective-permute-done.3 = bf16[32,4096]{1,0:T(8,128)(2,1)S(1)} collective-permute-done((bf16[32,4096]{1,0:T(8,128)(2,1)S(1)}, bf16[32,4096]{1,0:T(8,128)(2,1)S(1)}, u32[]{:S(2)}, u32[]{:S(2)}) %collective-permute-start.3) | collective-permute-done | bytes 262176 | tf_op jit(solution)/shard_map/ppermute | solution.py:222
  20.0 0.0 copy-start
  20.0 0.8 copy-done
  20.8 1.0 shard_map.77.tokens
  21.8 7.1 %shard_map.81 = f32[2,64,1024]{2,1,0:T(8,128)S(1)} custom-call(s32[5]{0:T(128)S(1)} %stack.23.where, bf16[3,64,2048]{2,1,0:T(8,128)(2,1)S(1)} %shard_map.77.tokens, bf16[2048,4096]{1,0:T(8,128)(2,1)} %gate.7, bf16[2048,4096]{1,0:T(8,128)(2,1)} %up.7, s32[32,4096]{1,0:T(8,128)} %gate_code.7, s32[32,4096]{1,0:T(8,128)} %up_code.7), custom_call_target="tpu_custom_call" | custom-call | flops 1610612736 | bytes 8388608 | tf_op jit(solution)/shard_map/pallas_call | solution.py:24
  28.9 0.1 collective-permute-start.5
  29.0 7.1 %shard_map.79 = f32[2,64,1024]{2,1,0:T(8,128)S(1)} custom-call(s32[5]{0:T(128)S(1)} %stack.23.where, bf16[3,64,2048]{2,1,0:T(8,128)(2,1)S(1)} %shard_map.77.tokens, bf16[2048,4096]{1,0:T(8,128)(2,1)} %gate.7, bf16[2048,4096]{1,0:T(8,128)(2,1)} %up.7, s32[32,4096]{1,0:T(8,128)} %gate_code.7, s32[32,4096]{1,0:T(8,128)} %up_code.7), custom_call_target="tpu_custom_call" | custom-call | flops 1610612736 | bytes 8388608 | tf_op jit(solution)/shard_map/pallas_call | solution.py:24
  36.1 0.6 collective-permute-start.4
  36.6 7.2 %shard_map.80 = f32[2,64,1024]{2,1,0:T(8,128)S(1)} custom-call(s32[5]{0:T(128)S(1)} %stack.23.where, bf16[3,64,2048]{2,1,0:T(8,128)(2,1)S(1)} %shard_map.77.tokens, bf16[2048,4096]{1,0:T(8,128)(2,1)} %gate.7, bf16[2048,4096]{1,0:T(8,128)(2,1)} %up.7, s32[32,4096]{1,0:T(8,128)} %gate_code.7, s32[32,4096]{1,0:T(8,128)} %up_code.7), custom_call_target="tpu_custom_call" | custom-call | flops 1610612736 | bytes 8388608 | tf_op jit(solution)/shard_map/pallas_call | solution.py:24
  43.9 0.0 collective-permute-done.5
  43.9 0.1 add.37
  43.9 1.6 %collective-permute-start.6 = (f32[2,64,1024]{2,1,0:T(8,128)S(1)}, f32[2,64,1024]{2,1,0:T(8,128)S(1)}, u32[]{:S(2)}, u32[]{:S(2)}) collective-permute-start(f32[2,64,1024]{2,1,0:T(8,128)S(1)} %add.37), channel_id=1, source_target_pairs={{0,2},{1,3},{2,0},{3,1},{4,6},{5,7},{6,4},{7,5},{8,10},{9,11},{10,... | collective-permute-start | bytes 1572872 | tf_op jit(solution)/shard_map/ppermute | solution.py:224
  45.5 7.1 %shard_map.78 = f32[2,64,1024]{2,1,0:T(8,128)S(1)} custom-call(s32[5]{0:T(128)S(1)} %stack.23.where, bf16[3,64,2048]{2,1,0:T(8,128)(2,1)S(1)} %shard_map.77.tokens, bf16[2048,4096]{1,0:T(8,128)(2,1)} %gate.7, bf16[2048,4096]{1,0:T(8,128)(2,1)} %up.7, s32[32,4096]{1,0:T(8,128)} %gate_code.7, s32[32,4096]{1,0:T(8,128)} %up_code.7), custom_call_target="tpu_custom_call" | custom-call | flops 1610612736 | bytes 8388608 | tf_op jit(solution)/shard_map/pallas_call | solution.py:24
  52.6 0.0 collective-permute-done.4
  52.6 5.3 %collective-permute-done.6 = f32[2,64,1024]{2,1,0:T(8,128)S(1)} collective-permute-done((f32[2,64,1024]{2,1,0:T(8,128)S(1)}, f32[2,64,1024]{2,1,0:T(8,128)S(1)}, u32[]{:S(2)}, u32[]{:S(2)}) %collective-permute-start.6) | collective-permute-done | bytes 524320 | tf_op jit(solution)/shard_map/ppermute | solution.py:224
  57.9 0.1 add_add_fusion
  58.0 0.1 fusion.1.own
  58.0 1.6 %collective-permute-start.7 = (bf16[64,1024]{1,0:T(8,128)(2,1)S(1)}, bf16[64,1024]{1,0:T(8,128)(2,1)S(1)}, u32[]{:S(2)}, u32[]{:S(2)}) collective-permute-start(bf16[64,1024]{1,0:T(8,128)(2,1)S(1)} %fusion.1.own), channel_id=1, source_target_pairs={{0,2},{1,3},{2,0},{3,1},{4,6},{5,7},{6,4},{7,5},{8,10},{9,11},{10,... | collective-permute-start | bytes 393224 | tf_op jit(solution)/shard_map/ppermute | solution.py:224
  59.6 0.0 collective-permute-start.9
  59.6 3.5 %collective-permute-done.7.own = bf16[64,1024]{1,0:T(8,128)(2,1)S(1)} collective-permute-done((bf16[64,1024]{1,0:T(8,128)(2,1)S(1)}, bf16[64,1024]{1,0:T(8,128)(2,1)S(1)}, u32[]{:S(2)}, u32[]{:S(2)}) %collective-permute-start.7) | collective-permute-done | bytes 131104 | tf_op jit(solution)/shard_map/ppermute | solution.py:224
  63.1 0.0 collective-permute-start.8
  63.1 6.5 %shard_map.83.weights = bf16[2048,4096]{1,0:T(8,128)(2,1)S(1)} custom-call(s32[5]{0:T(128)S(1)} %stack.23.where, bf16[4096,4096]{1,0:T(8,128)(2,1)} %source.3), custom_call_target="tpu_custom_call" | custom-call | bytes 16777216 | tf_op jit(solution)/shard_map/pallas_call | solution.py:24
  69.6 6.5 %shard_map.82.weights = bf16[2048,4096]{1,0:T(8,128)(2,1)S(1)} custom-call(s32[5]{0:T(128)S(1)} %stack.23.where, bf16[4096,4096]{1,0:T(8,128)(2,1)} %source.3), custom_call_target="tpu_custom_call" | custom-call | bytes 16777216 | tf_op jit(solution)/shard_map/pallas_call | solution.py:24
  76.0 0.0 collective-permute-done.9.beside
  76.1 3.6 %shard_map.84.rest_0_ = f32[64,4096]{1,0:T(8,128)S(1)} custom-call(s32[5]{0:T(128)S(1)} %stack.23.where, bf16[64,1024]{1,0:T(8,128)(2,1)S(1)} %fusion.1.own, bf16[64,1024]{1,0:T(8,128)(2,1)S(1)} %collective-permute-done.9.beside, bf16[2048,4096]{1,0:T(8,128)(2,1)S(1)} %shard_map.83.weights), custom_call_target="tpu_custom_call" | custom-call | flops 1073741824 | bytes 16777216 | tf_op jit(solution)/shard_map/pallas_call | solution.py:24
  79.6 0.0 collective-permute-done.8.beside
  79.6 2.1 %shard_map.86 = bf16[64,2048]{1,0:T(8,128)(2,1)S(1)} custom-call(s32[5]{0:T(128)S(1)} %stack.23.where, bf16[64,1024]{1,0:T(8,128)(2,1)S(1)} %collective-permute-done.7.own, bf16[64,1024]{1,0:T(8,128)(2,1)S(1)} %collective-permute-done.8.beside, bf16[2048,4096]{1,0:T(8,128)(2,1)S(1)} %shard_map.82.weights, f32[64,4096]{1,0:T(8,128)S(1)} %shard_map.84.rest_0_), custom_call_target="tpu_custom_call" | custom-call | flops 536870912 | bytes 8388608 | tf_op jit(solution)/shard_map/pallas_call | solution.py:24
  81.8 1.6 %collective-permute-start.10 = (bf16[64,2048]{1,0:T(8,128)(2,1)S(1)}, bf16[64,2048]{1,0:T(8,128)(2,1)S(1)}, u32[]{:S(2)}, u32[]{:S(2)}) collective-permute-start(bf16[64,2048]{1,0:T(8,128)(2,1)S(1)} %shard_map.86), channel_id=1, source_target_pairs={{0,4},{4,0},{8,12},{12,8},{16,20},{20,16},{24,28},{28,24},{1,5},{5... | collective-permute-start | bytes 786440 | tf_op jit(solution)/shard_map/ppermute | solution.py:222
  83.4 2.1 %shard_map.85.mine = f32[64,2048]{1,0:T(8,128)S(1)} custom-call(s32[5]{0:T(128)S(1)} %stack.23.where, bf16[64,1024]{1,0:T(8,128)(2,1)S(1)} %collective-permute-done.7.own, bf16[64,1024]{1,0:T(8,128)(2,1)S(1)} %collective-permute-done.8.beside, bf16[2048,4096]{1,0:T(8,128)(2,1)S(1)} %shard_map.82.weights, f32[64,4096]{1,0:T(8,128)S(1)} %shard_map.84.rest_0_), custom_call_target="tpu_custom_call" | custom-call | flops 536870912 | bytes 8388608 | tf_op jit(solution)/shard_map/pallas_call | solution.py:24
  85.5 5.1 %collective-permute-done.10.theirs = bf16[64,2048]{1,0:T(8,128)(2,1)S(1)} collective-permute-done((bf16[64,2048]{1,0:T(8,128)(2,1)S(1)}, bf16[64,2048]{1,0:T(8,128)(2,1)S(1)}, u32[]{:S(2)}, u32[]{:S(2)}) %collective-permute-start.10) | collective-permute-done | bytes 262176 | tf_op jit(solution)/shard_map/ppermute | solution.py:222
  90.6 0.6 shard_map.87
  91.2 0.8 collective-permute-start.11
  92.0 1.5 %collective-permute-start.12 = (bf16[16,2048]{1,0:T(8,128)(2,1)S(1)}, bf16[16,2048]{1,0:T(8,128)(2,1)S(1)}, u32[]{:S(2)}, u32[]{:S(2)}) collective-permute-start(bf16[16,2048]{1,0:T(8,128)(2,1)S(1)} %get-tuple-element.10), channel_id=1, source_target_pairs={{0,16},{4,20},{8,24},{12,28},{16,0},{20,4},{24,8},{28,12},{1,17},{... | collective-permute-start | bytes 196616 | tf_op jit(solution)/shard_map/ppermute | solution.py:225
  93.5 2.1 %collective-permute-start.13 = (bf16[16,2048]{1,0:T(8,128)(2,1)S(1)}, bf16[16,2048]{1,0:T(8,128)(2,1)S(1)}, u32[]{:S(2)}, u32[]{:S(2)}) collective-permute-start(bf16[16,2048]{1,0:T(8,128)(2,1)S(1)} %get-tuple-element.11), channel_id=1, source_target_pairs={{0,24},{4,28},{8,16},{12,20},{16,8},{20,12},{24,0},{28,4},{1,25},{... | collective-permute-start | bytes 196616 | tf_op jit(solution)/shard_map/ppermute | solution.py:225
  95.6 0.6 collective-permute-done.11.refs_1_
  96.2 3.8 %collective-permute-done.12.refs_2_ = bf16[16,2048]{1,0:T(8,128)(2,1)S(1)} collective-permute-done((bf16[16,2048]{1,0:T(8,128)(2,1)S(1)}, bf16[16,2048]{1,0:T(8,128)(2,1)S(1)}, u32[]{:S(2)}, u32[]{:S(2)}) %collective-permute-start.12) | collective-permute-done | bytes 65568 | tf_op jit(solution)/shard_map/ppermute | solution.py:225
  100.0 0.0 collective-permute-done.13.refs_3_
  100.0 0.6 shard_map.88.refs_0_
  100.6 1.3 collective-permute-start.14
  101.9 1.7 %collective-permute-start.15 = (bf16[16,2048]{1,0:T(8,128)(2,1)S(1)}, bf16[16,2048]{1,0:T(8,128)(2,1)S(1)}, u32[]{:S(2)}, u32[]{:S(2)}) collective-permute-start(bf16[16,2048]{1,0:T(8,128)(2,1)S(1)} %shard_map.88.refs_0_), channel_id=1, source_target_pairs={{0,16},{4,20},{8,24},{12,28},{16,0},{20,4},{24,8},{28,12},{1,17},{... | collective-permute-start | bytes 196616 | tf_op jit(solution)/shard_map/ppermute | solution.py:225
  103.6 1.4 collective-permute-start.16
  105.0 0.6 collective-permute-done.14.refs_1_
  105.6 3.1 %collective-permute-done.15.refs_2_ = bf16[16,2048]{1,0:T(8,128)(2,1)S(1)} collective-permute-done((bf16[16,2048]{1,0:T(8,128)(2,1)S(1)}, bf16[16,2048]{1,0:T(8,128)(2,1)S(1)}, u32[]{:S(2)}, u32[]{:S(2)}) %collective-permute-start.15) | collective-permute-done | bytes 65568 | tf_op jit(solution)/shard_map/ppermute | solution.py:225
  108.7 1.1 collective-permute-done.16.refs_3_
  109.8 0.6 shard_map.89.own
  110.4 3.4 %collective-permute-start.18 = (bf16[64,2048]{1,0:T(8,128)(2,1)S(1)}, bf16[64,2048]{1,0:T(8,128)(2,1)S(1)}, u32[]{:S(2)}, u32[]{:S(2)}) collective-permute-start(bf16[64,2048]{1,0:T(8,128)(2,1)S(1)} %broadcast_select_fusion), channel_id=1, source_target_pairs={{0,2},{4,6},{9,11},{13,15},{18,16},{22,20},{27,25},{31,29}} | collective-permute-start | bytes 786440 | tf_op jit(solution)/shard_map/ppermute | solution.py:328
  113.8 3.9 %collective-permute-done.18 = bf16[64,2048]{1,0:T(8,128)(2,1)S(1)} collective-permute-done((bf16[64,2048]{1,0:T(8,128)(2,1)S(1)}, bf16[64,2048]{1,0:T(8,128)(2,1)S(1)}, u32[]{:S(2)}, u32[]{:S(2)}) %collective-permute-start.18) | collective-permute-done | bytes 262176 | tf_op jit(solution)/shard_map/ppermute | solution.py:328
  117.7 0.1 collective-permute-start.19
  117.8 1.6 %collective-permute-start.17 = (bf16[64,2048]{1,0:T(8,128)(2,1)S(1)}, bf16[64,2048]{1,0:T(8,128)(2,1)S(1)}, u32[]{:S(2)}, u32[]{:S(2)}) collective-permute-start(bf16[64,2048]{1,0:T(8,128)(2,1)S(1)} %shard_map.89.own), channel_id=1, source_target_pairs={{0,4},{4,0},{8,12},{12,8},{16,20},{20,16},{24,28},{28,24},{1,5},{5... | collective-permute-start | bytes 786440 | tf_op jit(solution)/shard_map/ppermute | solution.py:222
  119.4 0.0 collective-permute-done.19
  119.4 7.1 %collective-permute-done.17.other = bf16[64,2048]{1,0:T(8,128)(2,1)S(1)} collective-permute-done((bf16[64,2048]{1,0:T(8,128)(2,1)S(1)}, bf16[64,2048]{1,0:T(8,128)(2,1)S(1)}, u32[]{:S(2)}, u32[]{:S(2)}) %collective-permute-start.17) | collective-permute-done | bytes 262176 | tf_op jit(solution)/shard_map/ppermute | solution.py:222
  126.5 13.0 %shard_map.90 = (f32[4096,2048]{1,0:T(8,128)}, bf16[8,4096]{1,0:T(8,128)(2,1)}) custom-call(s32[5]{0:T(128)S(1)} %stack.23.where, bf16[64,2048]{1,0:T(8,128)(2,1)S(1)} %shard_map.89.own, bf16[64,2048]{1,0:T(8,128)(2,1)S(1)} %collective-permute-done.17.other, bf16[64,2048]{1,0:T(8,128)(2,1)S(1)} %select_add_fusion.columns), custom_call_target="tpu_custom_call" | custom-call | flops 1073741824 | bytes 33554432 | tf_op jit(solution)/shard_map/pallas_call | solution.py:24
  (4 shorter events, 0.1 us)
Async XLA Ops:
  0.6 5.7 %collective-permute-start = (bf16[8,4096]{1,0:T(8,128)(2,1)}, bf16[8,4096]{1,0:T(8,128)(2,1)S(1)}, u32[]{:S(2)}, u32[]{:S(2)}) collective-permute-start(bf16[8,4096]{1,0:T(8,128)(2,1)} %refs_0_.1), channel_id=1, source_target_pairs={{0,8},{4,12},{8,0},{12,4},{16,24},{20,28},{24,16},{28,20},{1,9},{5... | collective-permute-start | bytes 196616 | tf_op jit(solution)/shard_map/ppermute | solution.py:225
  3.7 7.5 %collective-permute-start.1 = (bf16[8,4096]{1,0:T(8,128)(2,1)}, bf16[8,4096]{1,0:T(8,128)(2,1)S(1)}, u32[]{:S(2)}, u32[]{:S(2)}) collective-permute-start(bf16[8,4096]{1,0:T(8,128)(2,1)} %refs_0_.1), channel_id=1, source_target_pairs={{0,16},{4,20},{8,24},{12,28},{16,0},{20,4},{24,8},{28,12},{1,17},{... | collective-permute-start | bytes 196616 | tf_op jit(solution)/shard_map/ppermute | solution.py:225
  6.3 6.3 %collective-permute-start.2 = (bf16[8,4096]{1,0:T(8,128)(2,1)}, bf16[8,4096]{1,0:T(8,128)(2,1)S(1)}, u32[]{:S(2)}, u32[]{:S(2)}) collective-permute-start(bf16[8,4096]{1,0:T(8,128)(2,1)} %refs_0_.1), channel_id=1, source_target_pairs={{0,24},{4,28},{8,16},{12,20},{16,8},{20,12},{24,0},{28,4},{1,25},{... | collective-permute-start | bytes 196616 | tf_op jit(solution)/shard_map/ppermute | solution.py:225
  13.5 6.5 %collective-permute-start.3 = (bf16[32,4096]{1,0:T(8,128)(2,1)S(1)}, bf16[32,4096]{1,0:T(8,128)(2,1)S(1)}, u32[]{:S(2)}, u32[]{:S(2)}) collective-permute-start(bf16[32,4096]{1,0:T(8,128)(2,1)S(1)} %pad_maximum_fusion), channel_id=1, source_target_pairs={{0,4},{4,0},{8,12},{12,8},{16,20},{20,16},{24,28},{28,24},{1,5},{5... | collective-permute-start | bytes 786440 | tf_op jit(solution)/shard_map/ppermute | solution.py:222
  20.0 0.8 copy-start
  28.9 15.0 %collective-permute-start.5 = (f32[2,64,1024]{2,1,0:T(8,128)S(1)}, f32[2,64,1024]{2,1,0:T(8,128)S(1)}, u32[]{:S(2)}, u32[]{:S(2)}) collective-permute-start(f32[2,64,1024]{2,1,0:T(8,128)S(1)} %shard_map.81), channel_id=1, source_target_pairs={{0,1},{1,0},{2,3},{3,2},{4,5},{5,4},{6,7},{7,6},{8,9},{9,8},{10,11... | collective-permute-start | bytes 1572872 | tf_op jit(solution)/shard_map/ppermute | solution.py:223
  36.1 16.5 %collective-permute-start.4 = (f32[2,64,1024]{2,1,0:T(8,128)S(1)}, f32[2,64,1024]{2,1,0:T(8,128)S(1)}, u32[]{:S(2)}, u32[]{:S(2)}) collective-permute-start(f32[2,64,1024]{2,1,0:T(8,128)S(1)} %shard_map.79), channel_id=1, source_target_pairs={{0,1},{1,0},{2,3},{3,2},{4,5},{5,4},{6,7},{7,6},{8,9},{9,8},{10,11... | collective-permute-start | bytes 1572872 | tf_op jit(solution)/shard_map/ppermute | solution.py:223
  43.9 13.9 %collective-permute-start.6 = (f32[2,64,1024]{2,1,0:T(8,128)S(1)}, f32[2,64,1024]{2,1,0:T(8,128)S(1)}, u32[]{:S(2)}, u32[]{:S(2)}) collective-permute-start(f32[2,64,1024]{2,1,0:T(8,128)S(1)} %add.37), channel_id=1, source_target_pairs={{0,2},{1,3},{2,0},{3,1},{4,6},{5,7},{6,4},{7,5},{8,10},{9,11},{10,... | collective-permute-start | bytes 1572872 | tf_op jit(solution)/shard_map/ppermute | solution.py:224
  58.0 5.0 %collective-permute-start.7 = (bf16[64,1024]{1,0:T(8,128)(2,1)S(1)}, bf16[64,1024]{1,0:T(8,128)(2,1)S(1)}, u32[]{:S(2)}, u32[]{:S(2)}) collective-permute-start(bf16[64,1024]{1,0:T(8,128)(2,1)S(1)} %fusion.1.own), channel_id=1, source_target_pairs={{0,2},{1,3},{2,0},{3,1},{4,6},{5,7},{6,4},{7,5},{8,10},{9,11},{10,... | collective-permute-start | bytes 393224 | tf_op jit(solution)/shard_map/ppermute | solution.py:224
  59.6 16.4 %collective-permute-start.9 = (bf16[64,1024]{1,0:T(8,128)(2,1)S(1)}, bf16[64,1024]{1,0:T(8,128)(2,1)S(1)}, u32[]{:S(2)}, u32[]{:S(2)}) collective-permute-start(bf16[64,1024]{1,0:T(8,128)(2,1)S(1)} %fusion.1.own), channel_id=1, source_target_pairs={{0,1},{1,0},{2,3},{3,2},{4,5},{5,4},{6,7},{7,6},{8,9},{9,8},{10,11... | collective-permute-start | bytes 393224 | tf_op jit(solution)/shard_map/ppermute | solution.py:223
  63.1 16.6 %collective-permute-start.8 = (bf16[64,1024]{1,0:T(8,128)(2,1)S(1)}, bf16[64,1024]{1,0:T(8,128)(2,1)S(1)}, u32[]{:S(2)}, u32[]{:S(2)}) collective-permute-start(bf16[64,1024]{1,0:T(8,128)(2,1)S(1)} %collective-permute-done.7.own), channel_id=1, source_target_pairs={{0,1},{1,0},{2,3},{3,2},{4,5},{5,4},{6,7},{7,6},{8,9},{9,8},{10,11... | collective-permute-start | bytes 393224 | tf_op jit(solution)/shard_map/ppermute | solution.py:223
  81.8 8.8 %collective-permute-start.10 = (bf16[64,2048]{1,0:T(8,128)(2,1)S(1)}, bf16[64,2048]{1,0:T(8,128)(2,1)S(1)}, u32[]{:S(2)}, u32[]{:S(2)}) collective-permute-start(bf16[64,2048]{1,0:T(8,128)(2,1)S(1)} %shard_map.86), channel_id=1, source_target_pairs={{0,4},{4,0},{8,12},{12,8},{16,20},{20,16},{24,28},{28,24},{1,5},{5... | collective-permute-start | bytes 786440 | tf_op jit(solution)/shard_map/ppermute | solution.py:222
  91.2 5.0 %collective-permute-start.11 = (bf16[16,2048]{1,0:T(8,128)(2,1)S(1)}, bf16[16,2048]{1,0:T(8,128)(2,1)S(1)}, u32[]{:S(2)}, u32[]{:S(2)}) collective-permute-start(bf16[16,2048]{1,0:T(8,128)(2,1)S(1)} %get-tuple-element.9), channel_id=1, source_target_pairs={{0,8},{4,12},{8,0},{12,4},{16,24},{20,28},{24,16},{28,20},{1,9},{5... | collective-permute-start | bytes 196616 | tf_op jit(solution)/shard_map/ppermute | solution.py:225
  92.0 8.0 %collective-permute-start.12 = (bf16[16,2048]{1,0:T(8,128)(2,1)S(1)}, bf16[16,2048]{1,0:T(8,128)(2,1)S(1)}, u32[]{:S(2)}, u32[]{:S(2)}) collective-permute-start(bf16[16,2048]{1,0:T(8,128)(2,1)S(1)} %get-tuple-element.10), channel_id=1, source_target_pairs={{0,16},{4,20},{8,24},{12,28},{16,0},{20,4},{24,8},{28,12},{1,17},{... | collective-permute-start | bytes 196616 | tf_op jit(solution)/shard_map/ppermute | solution.py:225
  93.5 6.4 %collective-permute-start.13 = (bf16[16,2048]{1,0:T(8,128)(2,1)S(1)}, bf16[16,2048]{1,0:T(8,128)(2,1)S(1)}, u32[]{:S(2)}, u32[]{:S(2)}) collective-permute-start(bf16[16,2048]{1,0:T(8,128)(2,1)S(1)} %get-tuple-element.11), channel_id=1, source_target_pairs={{0,24},{4,28},{8,16},{12,20},{16,8},{20,12},{24,0},{28,4},{1,25},{... | collective-permute-start | bytes 196616 | tf_op jit(solution)/shard_map/ppermute | solution.py:225
  100.6 5.0 %collective-permute-start.14 = (bf16[16,2048]{1,0:T(8,128)(2,1)S(1)}, bf16[16,2048]{1,0:T(8,128)(2,1)S(1)}, u32[]{:S(2)}, u32[]{:S(2)}) collective-permute-start(bf16[16,2048]{1,0:T(8,128)(2,1)S(1)} %shard_map.88.refs_0_), channel_id=1, source_target_pairs={{0,8},{4,12},{8,0},{12,4},{16,24},{20,28},{24,16},{28,20},{1,9},{5... | collective-permute-start | bytes 196616 | tf_op jit(solution)/shard_map/ppermute | solution.py:225
  101.9 6.8 %collective-permute-start.15 = (bf16[16,2048]{1,0:T(8,128)(2,1)S(1)}, bf16[16,2048]{1,0:T(8,128)(2,1)S(1)}, u32[]{:S(2)}, u32[]{:S(2)}) collective-permute-start(bf16[16,2048]{1,0:T(8,128)(2,1)S(1)} %shard_map.88.refs_0_), channel_id=1, source_target_pairs={{0,16},{4,20},{8,24},{12,28},{16,0},{20,4},{24,8},{28,12},{1,17},{... | collective-permute-start | bytes 196616 | tf_op jit(solution)/shard_map/ppermute | solution.py:225
  103.6 6.2 %collective-permute-start.16 = (bf16[16,2048]{1,0:T(8,128)(2,1)S(1)}, bf16[16,2048]{1,0:T(8,128)(2,1)S(1)}, u32[]{:S(2)}, u32[]{:S(2)}) collective-permute-start(bf16[16,2048]{1,0:T(8,128)(2,1)S(1)} %shard_map.88.refs_0_), channel_id=1, source_target_pairs={{0,24},{4,28},{8,16},{12,20},{16,8},{20,12},{24,0},{28,4},{1,25},{... | collective-permute-start | bytes 196616 | tf_op jit(solution)/shard_map/ppermute | solution.py:225
  110.4 7.3 %collective-permute-start.18 = (bf16[64,2048]{1,0:T(8,128)(2,1)S(1)}, bf16[64,2048]{1,0:T(8,128)(2,1)S(1)}, u32[]{:S(2)}, u32[]{:S(2)}) collective-permute-start(bf16[64,2048]{1,0:T(8,128)(2,1)S(1)} %broadcast_select_fusion), channel_id=1, source_target_pairs={{0,2},{4,6},{9,11},{13,15},{18,16},{22,20},{27,25},{31,29}} | collective-permute-start | bytes 786440 | tf_op jit(solution)/shard_map/ppermute | solution.py:328
  117.7 1.7 %collective-permute-start.19 = (bf16[64,2048]{1,0:T(8,128)(2,1)S(1)}, bf16[64,2048]{1,0:T(8,128)(2,1)S(1)}, u32[]{:S(2)}, u32[]{:S(2)}) collective-permute-start(bf16[64,2048]{1,0:T(8,128)(2,1)S(1)} %fusion.3), channel_id=1, source_target_pairs={{0,1},{1,0},{2,3},{3,2},{4,5},{5,4},{6,7},{7,6},{8,9},{9,8},{10,11... | collective-permute-start | bytes 786440 | tf_op jit(solution)/shard_map/ppermute | solution.py:223
  117.8 8.7 %collective-permute-start.17 = (bf16[64,2048]{1,0:T(8,128)(2,1)S(1)}, bf16[64,2048]{1,0:T(8,128)(2,1)S(1)}, u32[]{:S(2)}, u32[]{:S(2)}) collective-permute-start(bf16[64,2048]{1,0:T(8,128)(2,1)S(1)} %shard_map.89.own), channel_id=1, source_target_pairs={{0,4},{4,0},{8,12},{12,8},{16,20},{20,16},{24,28},{28,24},{1,5},{5... | collective-permute-start | bytes 786440 | tf_op jit(solution)/shard_map/ppermute | solution.py:222
